TPU v7x, 32 devices: a whole 2x2x4 slice. The times are simulated.
32 devices in a mesh: tm: 2 (over core), station: 4 (over y, x), channel: 4 (over z).
Axes of the slice: x: 2, y: 2, z: 4, core: 2. Of those that a mesh axis runs over, the one named last changes fastest.
Arguments:
- voltages: bfloat16 [2, 32, 2, 512, 512], P(None, 'channel', None, 'station', 'tm'), may hold values from -64 to 64
- start_seed: int32 [2, 32, 4, 2, 512], P(None, 'channel', None, None, 'station'), may hold values from -8 to 8
- beam_phase: int32 [512, 512], replicated, may hold values from 0 to 1023
- station_delay: int32 [512], replicated, may hold values from 0 to 1023
Outputs:
- beam_output: bfloat16 [2, 32, 2, 512, 512], P(None, 'channel', None, 'station', 'tm')
- subspace: float32 [2, 32, 4, 2, 512], P(None, 'channel', None, None, 'station')
All inputs are finite; a program needn't handle non-finite values.
Results may differ from a plain program's by a relative error of at most 0.017.
Values may be sent and summed in bfloat16 or wider, within the bound.
No kernel may reach another device: no remote copies, remote signals or barrier semaphores. Data moves between devices by JAX's collectives and lax.ppermute only.
A program may use at most 64 MiB of HBM per device.

v0:
```python
import functools

import jax
import jax.numpy as jnp
from jax import lax
from jax.experimental import pallas as pl
from jax.experimental.pallas import tpu as pltpu
from jax.sharding import PartitionSpec as P


ITERS = 3
PHASES = 1024
GROUP = ("tm", "station")


HIGH = lax.Precision.HIGHEST
VMEM = pltpu.MemorySpace.VMEM
SMEM = pltpu.MemorySpace.SMEM
HBM = pltpu.MemorySpace.HBM


def coefficients(subspace, voltage):
    real_v = voltage[0].astype(jnp.float32)
    imag_v = voltage[1].astype(jnp.float32)
    pattern = "...kpm,...pmt->...kt"
    real_sum = jnp.einsum(pattern, subspace[0], real_v, precision=HIGH) + jnp.einsum(
        pattern, subspace[1], imag_v, precision=HIGH
    )
    imag_sum = jnp.einsum(pattern, subspace[0], imag_v, precision=HIGH) - jnp.einsum(
        pattern, subspace[1], real_v, precision=HIGH
    )
    return jnp.stack([real_sum, imag_sum])


def applied(voltage, coefficient):
    real_v = voltage[0].astype(jnp.float32)
    imag_v = voltage[1].astype(jnp.float32)
    pattern = "...pmt,...kt->...kpm"
    real_sum = jnp.einsum(pattern, real_v, coefficient[0], precision=HIGH) + jnp.einsum(
        pattern, imag_v, coefficient[1], precision=HIGH
    )
    imag_sum = jnp.einsum(pattern, imag_v, coefficient[0], precision=HIGH) - jnp.einsum(
        pattern, real_v, coefficient[1], precision=HIGH
    )
    return jnp.stack([real_sum, imag_sum])


def gram_matrix(image_field):
    pattern = "...kpm,...lpm->...kl"
    real_sum = jnp.einsum(pattern, image_field[0], image_field[0], precision=HIGH) + jnp.einsum(
        pattern, image_field[1], image_field[1], precision=HIGH
    )
    imag_sum = jnp.einsum(pattern, image_field[0], image_field[1], precision=HIGH) - jnp.einsum(
        pattern, image_field[1], image_field[0], precision=HIGH
    )
    return jnp.stack([real_sum, imag_sum])


def inverse_factor(gram_real, gram_imag):
    rank_count = gram_real.shape[-1]
    nothing = jnp.zeros_like(gram_real[..., 0, 0])
    low_real = {}
    low_imag = {}
    for column in range(rank_count):
        diagonal = gram_real[..., column, column]
        for middle in range(column):
            diagonal = diagonal - low_real[column, middle] ** 2 - low_imag[column, middle] ** 2
        pivot_root = jnp.sqrt(diagonal)
        low_real[column, column] = pivot_root
        low_imag[column, column] = nothing
        for row_at in range(column + 1, rank_count):
            acc_real = gram_real[..., row_at, column]
            acc_imag = gram_imag[..., row_at, column]
            for middle in range(column):
                acc_real = acc_real - (
                    low_real[row_at, middle] * low_real[column, middle]
                    + low_imag[row_at, middle] * low_imag[column, middle]
                )
                acc_imag = acc_imag - (
                    low_imag[row_at, middle] * low_real[column, middle]
                    - low_real[row_at, middle] * low_imag[column, middle]
                )
            low_real[row_at, column] = acc_real / pivot_root
            low_imag[row_at, column] = acc_imag / pivot_root
    inv_real = {}
    inv_imag = {}
    for column in range(rank_count):
        inv_real[column, column] = 1.0 / low_real[column, column]
        inv_imag[column, column] = nothing
        for row_at in range(column + 1, rank_count):
            acc_real = nothing
            acc_imag = nothing
            for middle in range(column, row_at):
                acc_real = (
                    acc_real
                    + low_real[row_at, middle] * inv_real[middle, column]
                    - low_imag[row_at, middle] * inv_imag[middle, column]
                )
                acc_imag = (
                    acc_imag
                    + low_real[row_at, middle] * inv_imag[middle, column]
                    + low_imag[row_at, middle] * inv_real[middle, column]
                )
            inv_real[row_at, column] = -acc_real / low_real[row_at, row_at]
            inv_imag[row_at, column] = -acc_imag / low_real[row_at, row_at]
    span = range(rank_count)
    real_rows = [jnp.stack([inv_real.get((r, c), nothing) for c in span], axis=-1) for r in span]
    imag_rows = [jnp.stack([inv_imag.get((r, c), nothing) for c in span], axis=-1) for r in span]
    return (jnp.stack(real_rows, axis=-2), jnp.stack(imag_rows, axis=-2))


def orthonormal(image_field, sums):
    inv_real, inv_imag = inverse_factor(sums[0], sums[1])
    pattern = "...lpm,...kl->...kpm"
    real_sum = jnp.einsum(pattern, image_field[0], inv_real, precision=HIGH) + jnp.einsum(
        pattern, image_field[1], inv_imag, precision=HIGH
    )
    imag_sum = jnp.einsum(pattern, image_field[1], inv_real, precision=HIGH) - jnp.einsum(
        pattern, image_field[0], inv_imag, precision=HIGH
    )
    return jnp.stack([real_sum, imag_sum])


def project_out(voltage, subspace, coefficient):
    pattern = "...kpm,...kt->...pmt"
    real_sum = jnp.einsum(pattern, subspace[0], coefficient[0], precision=HIGH) - jnp.einsum(
        pattern, subspace[1], coefficient[1], precision=HIGH
    )
    imag_sum = jnp.einsum(pattern, subspace[0], coefficient[1], precision=HIGH) + jnp.einsum(
        pattern, subspace[1], coefficient[0], precision=HIGH
    )
    return jnp.stack(
        [voltage[0].astype(jnp.float32) - real_sum, voltage[1].astype(jnp.float32) - imag_sum]
    )


def beam_weights(phase_rows, delays, channel_numbers):
    summed = phase_rows + delays[None, :]
    index = summed[None, :, :] * (channel_numbers[:, None, None] + 1) % PHASES
    angle = index.astype(jnp.float32) * (2.0 * jnp.pi / PHASES)
    norming = 1.0 / jnp.sqrt(jnp.float32(delays.shape[0]))
    return (
        (jnp.cos(angle) * norming).astype(jnp.bfloat16),
        (-jnp.sin(angle) * norming).astype(jnp.bfloat16),
    )


def form_beams(real_w, imag_w, cleaned):
    dot = functools.partial(jnp.einsum, "cbm,cpmt->cpbt", preferred_element_type=jnp.float32)
    real_sum = dot(real_w, cleaned[0]) - dot(imag_w, cleaned[1])
    imag_sum = dot(real_w, cleaned[1]) + dot(imag_w, cleaned[0])
    return jnp.stack([real_sum, imag_sum])


def general_body(voltages, start_seed, beam_phase, station_delay):
    chan_count = voltages.shape[1]
    first_channel = lax.axis_index("channel") * chan_count
    channel_numbers = jnp.arange(chan_count, dtype=jnp.int32) + first_channel
    subspace = start_seed.astype(jnp.float32)
    for _ in range(ITERS):
        coefficient = lax.psum(
            coefficients(subspace, voltages).astype(jnp.bfloat16), "station"
        ).astype(jnp.float32)
        summed = lax.psum(applied(voltages, coefficient), "tm")
        sums = lax.psum(gram_matrix(summed), "station")
        subspace = orthonormal(summed, sums)
    coefficient = lax.psum(coefficients(subspace, voltages).astype(jnp.bfloat16), "station").astype(
        jnp.float32
    )
    cleaned = project_out(voltages, subspace, coefficient).astype(jnp.bfloat16)
    beam_count = beam_phase.shape[0] // lax.axis_size("station")
    first_beam = lax.axis_index("station") * beam_count
    phase_rows = lax.dynamic_slice_in_dim(beam_phase, first_beam, beam_count, 0)
    real_w, imag_w = beam_weights(phase_rows, station_delay, channel_numbers)
    beam_field = form_beams(real_w, imag_w, lax.all_gather(cleaned, "station", axis=3, tiled=True))
    power_part = jnp.sum(beam_field[0] ** 2 + beam_field[1] ** 2, axis=(0, 3))
    terms = chan_count * lax.axis_size("channel") * voltages.shape[4] * lax.axis_size("tm")
    beam_power = lax.psum(power_part, ("tm", "channel")) / terms
    rescale = lax.rsqrt(beam_power + 1e-06)
    beam_output = (beam_field * rescale[None, None, :, :, None]).astype(jnp.bfloat16)
    return (beam_output, subspace)


def room(mebibytes):
    return pltpu.CompilerParams(vmem_limit_bytes=mebibytes * 2**20)


def pack_kernel(me_ref, volt_ref, seed_ref, *refs):
    group = len(refs) - 3
    outs, (held_ref, sem, seed_sem) = refs[:group], refs[group:]
    me = me_ref[0]
    rows = volt_ref.shape[2]
    seeds = pltpu.make_async_copy(seed_ref, held_ref, seed_sem)
    seeds.start()
    copies = []
    for place in range(group):
        for part in range(2):
            copy = pltpu.make_async_copy(
                volt_ref.at[part, me ^ place],
                outs[place].at[pl.ds(part * rows, rows)],
                sem.at[place, part],
            )
            copy.start()
            copies.append(copy)
    rank = seed_ref.shape[2] // 2
    seeds.wait()
    for place in range(group):
        halves = []
        for part in range(2):
            pols = [
                held_ref[part, me ^ place, pl.ds(pol, rank, stride=2), :] for pol in range(2)
            ]
            halves.append(jnp.concatenate(pols, axis=1))
        start = jnp.concatenate(halves, axis=0).astype(jnp.float32)
        outs[place][2 * rows :, :] = start.astype(jnp.bfloat16)
    for copy in copies:
        copy.wait()


def cos_sin(index):
    quarter = PHASES // 4
    turn = (index + quarter // 2) // quarter if quarter & (quarter - 1) else (
        (index + quarter // 2) >> (quarter.bit_length() - 1)
    )
    rest = index - turn * quarter
    angle = rest.astype(jnp.float32) * (2.0 * jnp.pi / PHASES)
    square = angle * angle
    cos = 1.0 + square * (
        -0.5 + square * (1.0 / 24 + square * (-1.0 / 720 + square * (1.0 / 40320)))
    )
    sin = angle * (
        1.0 + square * (-1.0 / 6 + square * (1.0 / 120 + square * (-1.0 / 5040 + square * (1.0 / 362880))))
    )
    odd = (turn & 1) == 1
    base_cos = jnp.where(odd, sin, cos)
    base_sin = jnp.where(odd, cos, sin)
    flip_cos = ((turn + 1) & 2) == 2
    flip_sin = (turn & 2) == 2
    return jnp.where(flip_cos, -base_cos, base_cos), jnp.where(flip_sin, -base_sin, base_sin)


def weight_kernel(stations, scalars_ref, phase_ref, delay_ref, out_ref):
    mine, number = scalars_ref[0], scalars_ref[1]
    beams = phase_ref.shape[0]
    wide = stations
    places = phase_ref.shape[1] // wide
    norming = 1.0 / jnp.sqrt(jnp.float32(phase_ref.shape[1]))
    for place in range(places):
        column = pl.multiple_of((mine ^ place) * wide, wide)
        summed = phase_ref[:, pl.ds(column, wide)] + delay_ref[:, pl.ds(column, wide)]
        cos, sin = cos_sin((summed * number) & (PHASES - 1))
        real = (cos * norming).astype(jnp.bfloat16)
        imag = (-sin * norming).astype(jnp.bfloat16)
        first = pl.ds(place * wide, wide)
        second = pl.ds((places + place) * wide, wide)
        out_ref[:beams, first] = real
        out_ref[:beams, second] = -imag
        out_ref[beams:, first] = imag
        out_ref[beams:, second] = real


def split(value, count):
    parts = []
    for _ in range(count - 1):
        part = value.astype(jnp.bfloat16)
        parts.append(part)
        value = value - part.astype(jnp.float32)
    return parts + [value.astype(jnp.bfloat16)]


def nn(a, b):
    return lax.dot_general(a, b, (((1,), (0,)), ((), ())), preferred_element_type=jnp.float32)


def nt(a, b):
    return lax.dot_general(a, b, (((1,), (1,)), ((), ())), preferred_element_type=jnp.float32)


def tn(a, b):
    return lax.dot_general(a, b, (((0,), (0,)), ((), ())), preferred_element_type=jnp.float32)


def first_kernel(places, halves, rank, *refs):
    group = places * halves
    x, weight_ref, y = refs[:group], refs[group], refs[group + 1 : group + 1 + places]
    state_ref, rows_ref, sum_ref, clean_ref = refs[group + 1 + places :]
    inputs = (x[0].shape[0] - 2 * rank) // 2
    times = x[0].shape[1]
    rows = 2 * rank
    row_at = lax.broadcasted_iota(jnp.int32, (rows, 1), 0)
    top = row_at < rank
    sign = jnp.where(top, 1.0, -1.0).astype(jnp.float32)
    row_mod = jnp.where(top, row_at, row_at - rank)

    def swap(value):
        return jnp.concatenate([value[rank:], value[:rank]], axis=0)

    def fold(value):
        total = value[:rows]
        for piece in range(1, value.shape[0] // rows):
            total = total + value[piece * rows : (piece + 1) * rows]
        return total

    def coefficient_of(field, count):
        left = []
        for value in field:
            both = jnp.concatenate([sign * value, swap(value)], axis=1)
            left.append(jnp.concatenate(split(both, count), axis=0))
        out = []
        for half in range(halves):
            total = None
            for place in range(places):
                term = nn(left[place], x[half * places + place][: 2 * inputs, :])
                total = term if total is None else total + term
            out.append(fold(total))
        return out

    def image_of(coefficient):
        left = [jnp.concatenate(split(value, 3), axis=0) for value in coefficient]
        out = []
        for place in range(places):
            total = None
            for half in range(halves):
                term = nt(left[half], x[half * places + place][: 2 * inputs, :])
                total = term if total is None else total + term
            total = fold(total)
            out.append(swap(total[:, inputs:]) + sign * total[:, :inputs])
        return out

    def whitener(field):
        column = []
        for line in range(rows):
            total = None
            for value in field:
                term = jnp.sum(value * value[line : line + 1], axis=1, keepdims=True)
                total = term if total is None else total + term
            column.append(total)
        real, imag = [], []
        for line in range(rank):
            value = column[line] + swap(column[line + rank])
            real.append(jnp.where(top, value, swap(value)))
            value = column[line + rank] - swap(column[line])
            imag.append(jnp.where(top, value, swap(value)))
        zero = jnp.zeros((rows, 1), jnp.float32)
        inv_real = [jnp.where(row_mod == line, 1.0, zero) for line in range(rank)]
        inv_imag = [zero] * rank
        pivots = zero
        for step in range(rank):
            pivot = real[step][step : step + 1]
            pivots = jnp.where(row_mod == step, pivot, pivots)
            if step == rank - 1:
                break
            below = row_mod > step
            inverse = 1.0 / pivot
            mul_real = jnp.where(below, real[step] * inverse, 0.0)
            mul_imag = jnp.where(below, imag[step] * inverse, 0.0)

            def reduce(re, im):
                at_re, at_im = re[step : step + 1], im[step : step + 1]
                return (
                    re - (mul_real * at_re - mul_imag * at_im),
                    im - (mul_real * at_im + mul_imag * at_re),
                )

            for line in range(step + 1, rank):
                real[line], imag[line] = reduce(real[line], imag[line])
            for line in range(step + 1):
                inv_real[line], inv_imag[line] = reduce(inv_real[line], inv_imag[line])
        scale = 1.0 / jnp.sqrt(pivots)
        return [value * scale for value in inv_real], [value * scale for value in inv_imag]

    def basis(field, white):
        real, imag = white
        out = []
        for value in field:
            total = jnp.zeros_like(value)
            for line in range(rank):
                total = total + jnp.where(top, real[line], -imag[line]) * value[line : line + 1]
                total = total + jnp.where(top, imag[line], real[line]) * value[line + rank : line + rank + 1]
            out.append(total)
        return out

    def whitened(raw, white):
        real, imag = white
        out = []
        for value in raw:
            total = jnp.zeros_like(value)
            for line in range(rank):
                total = total + jnp.where(top, real[line], imag[line]) * value[line : line + 1]
                total = total + jnp.where(top, -imag[line], real[line]) * value[line + rank : line + rank + 1]
            out.append(total)
        return out

    start = [x[place][2 * inputs : 2 * inputs + rows, :].astype(jnp.float32) for place in range(places)]
    coefficient = coefficient_of(start, 1)
    for _ in range(ITERS):
        field = image_of(coefficient)
        raw = coefficient_of(field, 3)
        white = whitener(field)
        coefficient = whitened(raw, white)
    subspace = basis(field, white)

    for place in range(places):
        state_ref[:, place * inputs : (place + 1) * inputs] = subspace[place]
    for half in range(1, halves):
        first = places * inputs + (half - 1) * times
        state_ref[:, first : first + times] = coefficient[half]
    for place in range(places):
        rows_ref[place] = jnp.concatenate(split(subspace[place], 2), axis=0)
    form_half(x[:places], subspace, coefficient[0], weight_ref, clean_ref, y, rows_ref, sum_ref, True)


def form_half(x, subspace, coefficient, weight_ref, clean_ref, y, rows_ref, sum_ref, fresh):
    places, (rows, inputs), times = len(x), subspace[0].shape, coefficient.shape[1]
    rank = rows // 2
    pols = clean_ref.shape[0]
    wide = inputs // pols
    top = lax.broadcasted_iota(jnp.int32, (rows, 1), 0) < rank
    sign = jnp.where(top, 1.0, -1.0).astype(jnp.float32)
    turned = jnp.concatenate([coefficient[rank:], coefficient[:rank]], axis=0)
    high, low = split(jnp.concatenate([sign * coefficient, turned], axis=1), 2)
    right = jnp.concatenate([high, high, low], axis=0)
    for place in range(places):
        high, low = split(subspace[place], 2)
        gone = tn(jnp.concatenate([high, low, high], axis=0), right)
        for part in range(2):
            for pol in range(pols):
                at = part * inputs + pol * wide
                value = x[place][at : at + wide, :].astype(jnp.float32)
                value = value - gone[pol * wide : (pol + 1) * wide, part * times : (part + 1) * times]
                first = (part * places + place) * wide
                clean_ref[pol, first : first + wide, :] = value.astype(jnp.bfloat16)
    beams = weight_ref.shape[0] // (2 * places)
    for place in range(places):
        y[place][2 * inputs :, :] = rows_ref[place]
        for pol in range(pols):
            out = nn(weight_ref[2 * place * beams : 2 * (place + 1) * beams, :], clean_ref[pol])
            for part in range(2):
                at = part * inputs + pol * beams
                y[place][at : at + beams, :] = out[part * beams : (part + 1) * beams].astype(
                    jnp.bfloat16
                )
            square = out * out
            square = square[:beams] + square[beams:]
            lanes = square[:, :128]
            for lane in range(128, times, 128):
                lanes = lanes + square[:, lane : lane + 128]
            if fresh:
                sum_ref[place * pols + pol] = lanes
            else:
                sum_ref[place * pols + pol] += lanes


def second_kernel(places, *refs):
    x, (weight_ref, state_ref, rows_ref, before_ref) = refs[:places], refs[places : places + 4]
    y, (power_ref, clean_ref, sum_ref) = refs[places + 4 : 2 * places + 4], refs[2 * places + 4 :]
    inputs = clean_ref.shape[0] * clean_ref.shape[1] // (2 * places)
    subspace = [state_ref[:, place * inputs : (place + 1) * inputs] for place in range(places)]
    coefficient = state_ref[:, places * inputs :]
    sum_ref[...] = before_ref[...]
    form_half(x, subspace, coefficient, weight_ref, clean_ref, y, rows_ref, sum_ref, False)
    for line in range(sum_ref.shape[0]):
        power_ref[line : line + 1, :] = jnp.sum(sum_ref[line].T, axis=0, keepdims=True)


def finish_kernel(terms, me_ref, power_ref, *refs):
    *y, out_ref, base_ref, held, sem = refs
    me = me_ref[0]
    pols = power_ref.shape[0]
    beams = power_ref.shape[1]
    rescale = lax.rsqrt(power_ref[...] * (1.0 / terms) + 1e-06)
    square = jnp.concatenate([rescale, jnp.zeros((beams - pols, beams), jnp.float32)], axis=0).T
    scale = [jnp.broadcast_to(square[:, pol : pol + 1], (beams, y[0].shape[1])) for pol in range(pols)]
    inputs = pols * beams
    copies = []
    for place, source in enumerate(y):
        for part in range(2):
            for pol in range(pols):
                at = part * inputs + pol * beams
                value = source[at : at + beams, :].astype(jnp.float32) * scale[pol]
                held[place, part, pol * beams : (pol + 1) * beams, :] = value.astype(jnp.bfloat16)
            copy = pltpu.make_async_copy(
                held.at[place, part], out_ref.at[part, me ^ place], sem.at[place, part]
            )
            copy.start()
            copies.append(copy)
    rows = (y[0].shape[0] - 2 * inputs) // 2
    rank = rows // 2
    for place, source in enumerate(y):
        both = source[2 * inputs :, :].astype(jnp.float32)
        value = both[:rows] + both[rows:]
        for part in range(2):
            for pol in range(pols):
                base_ref[part, me ^ place, pl.ds(pol, rank, stride=pols), :] = value[
                    part * rank : (part + 1) * rank, pol * beams : (pol + 1) * beams
                ]
    for copy in copies:
        copy.wait()


def fast_body(voltages, start_seed, beam_phase, station_delay):
    _, chan_count, pols, stations, times = voltages.shape
    rank = start_seed.shape[2]
    places, halves = lax.axis_size("station"), lax.axis_size("tm")
    group = places * halves
    inputs = pols * stations
    station_at, tm_at = lax.axis_index("station"), lax.axis_index("tm")
    me = (tm_at * places + station_at).astype(jnp.int32)
    number = (lax.axis_index("channel") * chan_count + me + 1).astype(jnp.int32)
    me_array = me.reshape(1)
    rows = 2 * inputs + 4 * rank
    block = pltpu.VMEM((rows, times), jnp.bfloat16)
    raw_block = pltpu.VMEM((2 * inputs + 2 * rank, times), jnp.bfloat16)
    vmem = pl.BlockSpec(memory_space=VMEM)
    smem = pl.BlockSpec(memory_space=SMEM)
    hbm = pl.BlockSpec(memory_space=HBM)

    def swap_with(value, offset):
        pairs = [(at, at ^ offset) for at in range(group)]
        return lax.ppermute(value, GROUP, pairs)

    packed = pl.pallas_call(
        pack_kernel,
        out_shape=[raw_block] * group,
        in_specs=[smem, hbm, hbm],
        out_specs=[vmem] * group,
        scratch_shapes=[
            pltpu.VMEM((2, chan_count, rank * pols, stations), jnp.int32),
            pltpu.SemaphoreType.DMA((group, 2)),
            pltpu.SemaphoreType.DMA,
        ],
        compiler_params=room(6),
        cost_estimate=pl.CostEstimate(
            flops=0, transcendentals=0, bytes_accessed=4 * group * rows * times
        ),
    )(
        me_array,
        pltpu.with_memory_space_constraint(voltages.reshape(2, chan_count, inputs, times), HBM),
        pltpu.with_memory_space_constraint(
            start_seed.reshape(2, chan_count, rank * pols, stations), HBM
        ),
    )
    held = [packed[0]] + [swap_with(packed[o], o) for o in range(1, group)]

    total_stations = places * stations
    beams = beam_phase.shape[0] // places
    weights = pl.pallas_call(
        functools.partial(weight_kernel, stations),
        out_shape=jax.ShapeDtypeStruct((2 * places * beams, 2 * total_stations), jnp.bfloat16),
        grid_spec=pltpu.PrefetchScalarGridSpec(
            num_scalar_prefetch=1,
            grid=(places,),
            in_specs=[
                pl.BlockSpec((beams, total_stations), lambda at, ref: (ref[0] ^ at, 0)),
                pl.BlockSpec((1, total_stations), lambda at, ref: (0, 0)),
            ],
            out_specs=pl.BlockSpec((2 * beams, 2 * total_stations), lambda at, ref: (at, 0)),
        ),
        compiler_params=room(8),
        cost_estimate=pl.CostEstimate(
            flops=60 * beam_phase.size, transcendentals=0, bytes_accessed=12 * beam_phase.size
        ),
    )(
        jnp.stack([station_at.astype(jnp.int32), number]),
        pltpu.with_memory_space_constraint(beam_phase, HBM),
        pltpu.with_memory_space_constraint(station_delay.reshape(1, total_stations), HBM),
    )

    lines = places * pols
    lane_sums = pltpu.VMEM((lines, beams, 128), jnp.float32)
    clean = pltpu.VMEM((pols, 2 * total_stations, times), jnp.bfloat16)
    basis_rows = pltpu.VMEM((places, 4 * rank, times), jnp.bfloat16)
    work = 8 * beams * places * total_stations * pols * times
    *early, state, basis_rows_of, sums = pl.pallas_call(
        functools.partial(first_kernel, places, halves, rank),
        out_shape=[block] * places
        + [
            pltpu.VMEM((2 * rank, places * inputs + (halves - 1) * times), jnp.float32),
            basis_rows,
            lane_sums,
        ],
        in_specs=[vmem] * (group + 1),
        out_specs=[vmem] * (places + 3),
        scratch_shapes=[clean],
        compiler_params=room(16),
        cost_estimate=pl.CostEstimate(
            flops=2 * work, transcendentals=0, bytes_accessed=3 * group * rows * times
        ),
    )(*held, weights)
    back = [early[0]] + [swap_with(early[o], o) for o in range(1, places)]
    *late, power = pl.pallas_call(
        functools.partial(second_kernel, places),
        out_shape=[block] * places + [jax.ShapeDtypeStruct((lines, beams), jnp.float32)],
        in_specs=[vmem] * (places + 4),
        out_specs=[vmem] * (places + 1),
        scratch_shapes=[clean, lane_sums],
        compiler_params=room(12),
        cost_estimate=pl.CostEstimate(
            flops=work, transcendentals=0, bytes_accessed=2 * group * rows * times
        ),
    )(*held[places:], weights, state, basis_rows_of, sums)

    power = power.reshape(places, pols, beams)
    power = power + swap_with(power, places)
    power = functools.reduce(
        jnp.add,
        [power[0]] + [swap_with(power[o], o) for o in range(1, places)],
    )
    back += [swap_with(late[o], places + o) for o in range(places)]
    slices = lax.axis_size("channel")
    bit = 1
    while bit < slices:
        pairs = [(at, at ^ bit) for at in range(slices)]
        power = power + lax.ppermute(power, "channel", pairs)
        bit *= 2

    terms = float(chan_count * slices * times * halves)
    beam_output, subspace = pl.pallas_call(
        functools.partial(finish_kernel, terms),
        out_shape=[
            jax.ShapeDtypeStruct((2, chan_count, pols * beams, times), jnp.bfloat16),
            jax.ShapeDtypeStruct((2, chan_count, rank * pols, stations), jnp.float32),
        ],
        in_specs=[smem] + [vmem] * (group + 1),
        out_specs=[hbm, vmem],
        scratch_shapes=[
            pltpu.VMEM((group, 2, pols * beams, times), jnp.bfloat16),
            pltpu.SemaphoreType.DMA((group, 2)),
        ],
        compiler_params=room(10),
        cost_estimate=pl.CostEstimate(
            flops=0, transcendentals=0, bytes_accessed=4 * group * rows * times
        ),
    )(me_array, power, *back)
    return (
        beam_output.reshape(2, chan_count, pols, beams, times),
        subspace.reshape(2, chan_count, rank, pols, stations),
    )


def power_of_two(number):
    return number & (number - 1) == 0


def body(voltages, start_seed, beam_phase, station_delay):
    _, chan_count, pols, stations, times = voltages.shape
    places, halves, slices = (lax.axis_size(axis) for axis in ("station", "tm", "channel"))
    fits = (
        chan_count == places * halves
        and all(power_of_two(size) for size in (places, halves, slices))
        and halves == 2
        and pols == 2
        and stations == 128
        and times == pols * stations
        and start_seed.shape[2] == 4
        and beam_phase.shape[0] == places * stations
    )
    return (fast_body if fits else general_body)(voltages, start_seed, beam_phase, station_delay)


def solution(mesh):
    in_specs = (
        P(None, "channel", None, "station", "tm"),
        P(None, "channel", None, None, "station"),
        P(),
        P(),
    )
    out_specs = (
        P(None, "channel", None, "station", "tm"),
        P(None, "channel", None, None, "station"),
    )
    return jax.shard_map(body, mesh=mesh, in_specs=in_specs, out_specs=out_specs, check_vma=False)
```

profile of v0, /device:TPU:1, one launch (start us, length us, event | category | flops | bytes accessed | tf_op | source)
XLA Modules:
  0.0 81.9 jit_solution(14902014850039293128)
XLA Ops:
  0.6 1.8 %shard_map.59 = (bf16[520,256]{1,0:T(8,128)(2,1)S(1)}, bf16[520,256]{1,0:T(8,128)(2,1)S(1)}, bf16[520,256]{1,0:T(8,128)(2,1)S(1)}, bf16[520,256]{1,0:T(8,128)(2,...) custom-call(s32[1]{0:T(128)} %bitcast.me_ref, ...), custom_call_target="tpu_custom_call" | custom-call | bytes 4325376 | tf_op jit(solution)/shard_map/pallas_call | solution.py:522
  2.4 0.1 collective-permute-start
  2.5 2.7 %collective-permute-start.1 = (bf16[520,256]{1,0:T(8,128)(2,1)S(1)}, bf16[520,256]{1,0:T(8,128)(2,1)S(1)}, u32[]{:S(2)}, u32[]{:S(2)}) collective-permute-start(bf16[520,256]{1,0:T(8,128)(2,1)S(1)} %get-tuple-element.25), channel_id=1, source_target_pairs={{0,20},{4,16},{8,28},{12,24},{16,4},{20,0},{24,12},{28,8},{1,21},{... | collective-permute-start | bytes 798728 | tf_op jit(solution)/shard_map/ppermute | solution.py:520
  5.1 1.6 %collective-permute-start.2 = (bf16[520,256]{1,0:T(8,128)(2,1)S(1)}, bf16[520,256]{1,0:T(8,128)(2,1)S(1)}, u32[]{:S(2)}, u32[]{:S(2)}) collective-permute-start(bf16[520,256]{1,0:T(8,128)(2,1)S(1)} %get-tuple-element.26), channel_id=1, source_target_pairs={{0,24},{4,28},{8,16},{12,20},{16,8},{20,12},{24,0},{28,4},{1,25},{... | collective-permute-start | bytes 798728 | tf_op jit(solution)/shard_map/ppermute | solution.py:520
  6.7 0.0 collective-permute-start.3
  6.7 1.4 %collective-permute-start.4 = (bf16[520,256]{1,0:T(8,128)(2,1)S(1)}, bf16[520,256]{1,0:T(8,128)(2,1)S(1)}, u32[]{:S(2)}, u32[]{:S(2)}) collective-permute-start(bf16[520,256]{1,0:T(8,128)(2,1)S(1)} %get-tuple-element.29), channel_id=1, source_target_pairs={{0,4},{4,0},{8,12},{12,8},{16,20},{20,16},{24,28},{28,24},{1,5},{5... | collective-permute-start | bytes 798728 | tf_op jit(solution)/shard_map/ppermute | solution.py:520
  8.1 0.0 collective-permute-done.refs_4_.refs_0_
  8.1 1.2 %collective-permute-start.5 = (bf16[520,256]{1,0:T(8,128)(2,1)S(1)}, bf16[520,256]{1,0:T(8,128)(2,1)S(1)}, u32[]{:S(2)}, u32[]{:S(2)}) collective-permute-start(bf16[520,256]{1,0:T(8,128)(2,1)S(1)} %get-tuple-element.30), channel_id=1, source_target_pairs={{0,8},{4,12},{8,0},{12,4},{16,24},{20,28},{24,16},{28,20},{1,9},{5... | collective-permute-start | bytes 798728 | tf_op jit(solution)/shard_map/ppermute | solution.py:520
  9.3 3.1 %collective-permute-done.1.refs_5_.refs_1_ = bf16[520,256]{1,0:T(8,128)(2,1)S(1)} collective-permute-done((bf16[520,256]{1,0:T(8,128)(2,1)S(1)}, bf16[520,256]{1,0:T(8,128)(2,1)S(1)}, u32[]{:S(2)}, u32[]{:S(2)}) %collective-permute-start.1) | collective-permute-done | bytes 266272 | tf_op jit(solution)/shard_map/ppermute | solution.py:520
  12.4 2.7 %collective-permute-start.6 = (bf16[520,256]{1,0:T(8,128)(2,1)S(1)}, bf16[520,256]{1,0:T(8,128)(2,1)S(1)}, u32[]{:S(2)}, u32[]{:S(2)}) collective-permute-start(bf16[520,256]{1,0:T(8,128)(2,1)S(1)} %get-tuple-element.31), channel_id=1, source_target_pairs={{0,12},{4,8},{8,4},{12,0},{16,28},{20,24},{24,20},{28,16},{1,13},{... | collective-permute-start | bytes 798728 | tf_op jit(solution)/shard_map/ppermute | solution.py:520
  15.1 0.1 pad_add_fusion.scalars_ref
  15.2 3.8 %shard_map.60.refs_8_.refs_4_ = bf16[1024,1024]{1,0:T(8,128)(2,1)S(1)} custom-call(s32[2]{0:T(128)S(1)} %pad_add_fusion.scalars_ref, s32[512,512]{1,0:T(8,128)} %phase_ref.1, s32[1,512]{1,0:T(1,128)} %bitcast.27), custom_call_target="tpu_custom_call" | custom-call | flops 15728640 | bytes 3145728 | tf_op jit(solution)/shard_map/pallas_call | solution.py:547
  19.0 0.8 %collective-permute-done.2.refs_6_.refs_2_ = bf16[520,256]{1,0:T(8,128)(2,1)S(1)} collective-permute-done((bf16[520,256]{1,0:T(8,128)(2,1)S(1)}, bf16[520,256]{1,0:T(8,128)(2,1)S(1)}, u32[]{:S(2)}, u32[]{:S(2)}) %collective-permute-start.2) | collective-permute-done | bytes 266272 | tf_op jit(solution)/shard_map/ppermute | solution.py:520
  19.8 0.0 collective-permute-done.3.refs_7_.refs_3_
  19.8 3.5 %collective-permute-done.4.refs_1_ = bf16[520,256]{1,0:T(8,128)(2,1)S(1)} collective-permute-done((bf16[520,256]{1,0:T(8,128)(2,1)S(1)}, bf16[520,256]{1,0:T(8,128)(2,1)S(1)}, u32[]{:S(2)}, u32[]{:S(2)}) %collective-permute-start.4) | collective-permute-done | bytes 266272 | tf_op jit(solution)/shard_map/ppermute | solution.py:520
  23.3 7.4 %collective-permute-done.5.refs_2_ = bf16[520,256]{1,0:T(8,128)(2,1)S(1)} collective-permute-done((bf16[520,256]{1,0:T(8,128)(2,1)S(1)}, bf16[520,256]{1,0:T(8,128)(2,1)S(1)}, u32[]{:S(2)}, u32[]{:S(2)}) %collective-permute-start.5) | collective-permute-done | bytes 266272 | tf_op jit(solution)/shard_map/ppermute | solution.py:520
  30.7 0.0 collective-permute-done.6.refs_3_
  30.7 5.1 %shard_map.61 = (bf16[528,256]{1,0:T(8,128)(2,1)S(1)}, bf16[528,256]{1,0:T(8,128)(2,1)S(1)}, bf16[528,256]{1,0:T(8,128)(2,1)S(1)}, bf16[528,256]{1,0:T(8,128)(2,...) custom-call(bf16[520,256]{1,0:T(8,128)(2,1)S(1)} %get-tuple-element.28.refs_0_, ...), custom_call_target="tpu_custom_call" | custom-call | flops 2147483648 | bytes 3244032 | tf_op jit(solution)/shard_map/pallas_call | solution.py:574
  35.8 1.7 %shard_map.62 = (bf16[528,256]{1,0:T(8,128)(2,1)S(1)}, bf16[528,256]{1,0:T(8,128)(2,1)S(1)}, bf16[528,256]{1,0:T(8,128)(2,1)S(1)}, bf16[528,256]{1,0:T(8,128)(2,1)S(1)}, f32[8,128]{1,0:T(8,128)S(1)}) custom-call(bf16[520,256]{1,0:T(8,128)(2,1)S(1)} %collective-permute-done.refs_4_.refs_0_, bf16[520,256]{1,0:T(8,128)(2,1)S(1)} %collective-permute-done.1.refs_5_.refs_1_, ...), custom_call_target="tpu_custom_call" | custom-call | flops 1073741824 | bytes 2162688 | tf_op jit(solution)/shard_map/pallas_call | solution.py:591
  37.5 0.7 collective-permute-start.7
  38.2 0.1 collective-permute-start.16
  38.3 1.0 %collective-permute-start.17 = (bf16[528,256]{1,0:T(8,128)(2,1)S(1)}, bf16[528,256]{1,0:T(8,128)(2,1)S(1)}, u32[]{:S(2)}, u32[]{:S(2)}) collective-permute-start(bf16[528,256]{1,0:T(8,128)(2,1)S(1)} %get-tuple-element.41), channel_id=1, source_target_pairs={{0,20},{4,16},{8,28},{12,24},{16,4},{20,0},{24,12},{28,8},{1,21},{... | collective-permute-start | bytes 811016 | tf_op jit(solution)/shard_map/ppermute | solution.py:520
  39.3 0.0 collective-permute-done.7
  39.3 0.9 %collective-permute-start.8 = (f32[2,128]{1,0:T(2,128)S(1)}, f32[2,128]{1,0:T(2,128)S(1)}, u32[]{:S(2)}, u32[]{:S(2)}) collective-permute-start(f32[2,128]{1,0:T(2,128)S(1)} %get-tuple-element.46), channel_id=1, source_target_pairs={{0,4},{4,0},{8,12},{12,8},{16,20},{20,16},{24,28},{28,24},{1,5},{5... | collective-permute-start | bytes 3080 | tf_op jit(solution)/shard_map/ppermute | solution.py:520
  40.2 1.3 %collective-permute-start.10 = (f32[2,128]{1,0:T(2,128)S(1)}, f32[2,128]{1,0:T(2,128)S(1)}, u32[]{:S(2)}, u32[]{:S(2)}) collective-permute-start(f32[2,128]{1,0:T(2,128)S(1)} %get-tuple-element.47), channel_id=1, source_target_pairs={{0,12},{4,8},{8,4},{12,0},{16,28},{20,24},{24,20},{28,16},{1,13},{... | collective-permute-start | bytes 3080 | tf_op jit(solution)/shard_map/ppermute | solution.py:520
  41.5 0.5 collective-permute-start.9
  42.0 4.8 %collective-permute-done.8 = f32[2,128]{1,0:T(2,128)S(1)} collective-permute-done((f32[2,128]{1,0:T(2,128)S(1)}, f32[2,128]{1,0:T(2,128)S(1)}, u32[]{:S(2)}, u32[]{:S(2)}) %collective-permute-start.8) | collective-permute-done | bytes 1056 | tf_op jit(solution)/shard_map/ppermute | solution.py:520
  46.9 0.7 collective-permute-done.10
  47.6 0.0 collective-permute-done.9
  47.6 1.4 %collective-permute-start.11 = (f32[2,128]{1,0:T(2,128)S(1)}, f32[2,128]{1,0:T(2,128)S(1)}, u32[]{:S(2)}, u32[]{:S(2)}) collective-permute-start(f32[2,128]{1,0:T(2,128)S(1)} %fusion.2), channel_id=1, source_target_pairs={{0,1},{1,0},{2,3},{3,2},{4,5},{5,4},{6,7},{7,6},{8,9},{9,8},{10,11... | collective-permute-start | bytes 3080 | tf_op jit(solution)/shard_map/ppermute | solution.py:614
  49.0 1.1 %collective-permute-done.11 = f32[2,128]{1,0:T(2,128)S(1)} collective-permute-done((f32[2,128]{1,0:T(2,128)S(1)}, f32[2,128]{1,0:T(2,128)S(1)}, u32[]{:S(2)}, u32[]{:S(2)}) %collective-permute-start.11) | collective-permute-done | bytes 1056 | tf_op jit(solution)/shard_map/ppermute | solution.py:614
  50.1 2.3 %collective-permute-start.12 = (f32[2,128]{1,0:T(2,128)S(1)}, f32[2,128]{1,0:T(2,128)S(1)}, u32[]{:S(2)}, u32[]{:S(2)}) collective-permute-start(f32[2,128]{1,0:T(2,128)S(1)} %add.34), channel_id=1, source_target_pairs={{0,2},{1,3},{2,0},{3,1},{4,6},{5,7},{6,4},{7,5},{8,10},{9,11},{10,... | collective-permute-start | bytes 3080 | tf_op jit(solution)/shard_map/ppermute | solution.py:614
  52.4 2.5 %collective-permute-start.18 = (bf16[528,256]{1,0:T(8,128)(2,1)S(1)}, bf16[528,256]{1,0:T(8,128)(2,1)S(1)}, u32[]{:S(2)}, u32[]{:S(2)}) collective-permute-start(bf16[528,256]{1,0:T(8,128)(2,1)S(1)} %get-tuple-element.42), channel_id=1, source_target_pairs={{0,24},{4,28},{8,16},{12,20},{16,8},{20,12},{24,0},{28,4},{1,25},{... | collective-permute-start | bytes 811016 | tf_op jit(solution)/shard_map/ppermute | solution.py:520
  54.9 0.4 collective-permute-start.19
  55.3 0.0 collective-permute-done.12
  55.3 0.8 %collective-permute-start.13 = (bf16[528,256]{1,0:T(8,128)(2,1)S(1)}, bf16[528,256]{1,0:T(8,128)(2,1)S(1)}, u32[]{:S(2)}, u32[]{:S(2)}) collective-permute-start(bf16[528,256]{1,0:T(8,128)(2,1)S(1)} %get-tuple-element.37), channel_id=1, source_target_pairs={{0,4},{4,0},{8,12},{12,8},{16,20},{20,16},{24,28},{28,24},{1,5},{5... | collective-permute-start | bytes 811016 | tf_op jit(solution)/shard_map/ppermute | solution.py:520
  56.1 0.0 collective-permute-done.16.refs_4_
  56.1 1.2 %collective-permute-start.14 = (bf16[528,256]{1,0:T(8,128)(2,1)S(1)}, bf16[528,256]{1,0:T(8,128)(2,1)S(1)}, u32[]{:S(2)}, u32[]{:S(2)}) collective-permute-start(bf16[528,256]{1,0:T(8,128)(2,1)S(1)} %get-tuple-element.38), channel_id=1, source_target_pairs={{0,8},{4,12},{8,0},{12,4},{16,24},{20,28},{24,16},{28,20},{1,9},{5... | collective-permute-start | bytes 811016 | tf_op jit(solution)/shard_map/ppermute | solution.py:520
  57.3 0.0 collective-permute-done.17.refs_5_
  57.3 0.6 collective-permute-start.15
  58.0 9.3 %collective-permute-done.18.refs_6_ = bf16[528,256]{1,0:T(8,128)(2,1)S(1)} collective-permute-done((bf16[528,256]{1,0:T(8,128)(2,1)S(1)}, bf16[528,256]{1,0:T(8,128)(2,1)S(1)}, u32[]{:S(2)}, u32[]{:S(2)}) %collective-permute-start.18) | collective-permute-done | bytes 270368 | tf_op jit(solution)/shard_map/ppermute | solution.py:520
  67.3 0.0 collective-permute-done.19.refs_7_
  67.3 0.0 collective-permute-done.13.refs_1_
  67.3 12.1 %collective-permute-done.14.refs_2_ = bf16[528,256]{1,0:T(8,128)(2,1)S(1)} collective-permute-done((bf16[528,256]{1,0:T(8,128)(2,1)S(1)}, bf16[528,256]{1,0:T(8,128)(2,1)S(1)}, u32[]{:S(2)}, u32[]{:S(2)}) %collective-permute-start.14) | collective-permute-done | bytes 270368 | tf_op jit(solution)/shard_map/ppermute | solution.py:520
  79.4 0.0 collective-permute-done.15.refs_3_
  79.4 2.5 %shard_map.63 = (bf16[2,8,256,256]{3,2,1,0:T(8,128)(2,1)}, f32[2,8,8,128]{3,2,1,0:T(8,128)}) custom-call(s32[1]{0:T(128)} %bitcast.me_ref, f32[2,128]{1,0:T(2,128)S(1)} %add.35.power_ref, bf16[528,256]{1,0:T(8,128)(2,1)S(1)} %get-tuple-element.36.refs_0_, bf16[528,256]{1,0:T(8,128)(2,1)S(1)} %collective-permute-done.13.refs_1_, ...), custom_call_target="tpu_custom_call" | custom-call | bytes 4325376 | tf_op jit(solution)/shard_map/pallas_call | solution.py:618
  (5 shorter events, 0.0 us)
Async XLA Ops:
  2.4 5.7 %collective-permute-start = (bf16[520,256]{1,0:T(8,128)(2,1)S(1)}, bf16[520,256]{1,0:T(8,128)(2,1)S(1)}, u32[]{:S(2)}, u32[]{:S(2)}) collective-permute-start(bf16[520,256]{1,0:T(8,128)(2,1)S(1)} %get-tuple-element.24), channel_id=1, source_target_pairs={{0,16},{4,20},{8,24},{12,28},{16,0},{20,4},{24,8},{28,12},{1,17},{... | collective-permute-start | bytes 798728 | tf_op jit(solution)/shard_map/ppermute | solution.py:520
  2.5 9.9 %collective-permute-start.1 = (bf16[520,256]{1,0:T(8,128)(2,1)S(1)}, bf16[520,256]{1,0:T(8,128)(2,1)S(1)}, u32[]{:S(2)}, u32[]{:S(2)}) collective-permute-start(bf16[520,256]{1,0:T(8,128)(2,1)S(1)} %get-tuple-element.25), channel_id=1, source_target_pairs={{0,20},{4,16},{8,28},{12,24},{16,4},{20,0},{24,12},{28,8},{1,21},{... | collective-permute-start | bytes 798728 | tf_op jit(solution)/shard_map/ppermute | solution.py:520
  5.1 14.7 %collective-permute-start.2 = (bf16[520,256]{1,0:T(8,128)(2,1)S(1)}, bf16[520,256]{1,0:T(8,128)(2,1)S(1)}, u32[]{:S(2)}, u32[]{:S(2)}) collective-permute-start(bf16[520,256]{1,0:T(8,128)(2,1)S(1)} %get-tuple-element.26), channel_id=1, source_target_pairs={{0,24},{4,28},{8,16},{12,20},{16,8},{20,12},{24,0},{28,4},{1,25},{... | collective-permute-start | bytes 798728 | tf_op jit(solution)/shard_map/ppermute | solution.py:520
  6.7 13.1 %collective-permute-start.3 = (bf16[520,256]{1,0:T(8,128)(2,1)S(1)}, bf16[520,256]{1,0:T(8,128)(2,1)S(1)}, u32[]{:S(2)}, u32[]{:S(2)}) collective-permute-start(bf16[520,256]{1,0:T(8,128)(2,1)S(1)} %get-tuple-element.27), channel_id=1, source_target_pairs={{0,28},{4,24},{8,20},{12,16},{16,12},{20,8},{24,4},{28,0},{1,29},{... | collective-permute-start | bytes 798728 | tf_op jit(solution)/shard_map/ppermute | solution.py:520
  6.7 16.6 %collective-permute-start.4 = (bf16[520,256]{1,0:T(8,128)(2,1)S(1)}, bf16[520,256]{1,0:T(8,128)(2,1)S(1)}, u32[]{:S(2)}, u32[]{:S(2)}) collective-permute-start(bf16[520,256]{1,0:T(8,128)(2,1)S(1)} %get-tuple-element.29), channel_id=1, source_target_pairs={{0,4},{4,0},{8,12},{12,8},{16,20},{20,16},{24,28},{28,24},{1,5},{5... | collective-permute-start | bytes 798728 | tf_op jit(solution)/shard_map/ppermute | solution.py:520
  8.1 22.7 %collective-permute-start.5 = (bf16[520,256]{1,0:T(8,128)(2,1)S(1)}, bf16[520,256]{1,0:T(8,128)(2,1)S(1)}, u32[]{:S(2)}, u32[]{:S(2)}) collective-permute-start(bf16[520,256]{1,0:T(8,128)(2,1)S(1)} %get-tuple-element.30), channel_id=1, source_target_pairs={{0,8},{4,12},{8,0},{12,4},{16,24},{20,28},{24,16},{28,20},{1,9},{5... | collective-permute-start | bytes 798728 | tf_op jit(solution)/shard_map/ppermute | solution.py:520
  12.4 18.3 %collective-permute-start.6 = (bf16[520,256]{1,0:T(8,128)(2,1)S(1)}, bf16[520,256]{1,0:T(8,128)(2,1)S(1)}, u32[]{:S(2)}, u32[]{:S(2)}) collective-permute-start(bf16[520,256]{1,0:T(8,128)(2,1)S(1)} %get-tuple-element.31), channel_id=1, source_target_pairs={{0,12},{4,8},{8,4},{12,0},{16,28},{20,24},{24,20},{28,16},{1,13},{... | collective-permute-start | bytes 798728 | tf_op jit(solution)/shard_map/ppermute | solution.py:520
  37.5 1.8 %collective-permute-start.7 = (f32[4,2,128]{2,1,0:T(2,128)S(1)}, f32[4,2,128]{2,1,0:T(2,128)S(1)}, u32[]{:S(2)}, u32[]{:S(2)}) collective-permute-start(f32[4,2,128]{2,1,0:T(2,128)S(1)} %bitcast.23), channel_id=1, source_target_pairs={{0,16},{4,20},{8,24},{12,28},{16,0},{20,4},{24,8},{28,12},{1,17},{... | collective-permute-start | bytes 12296 | tf_op jit(solution)/shard_map/ppermute | solution.py:520
  38.2 17.9 %collective-permute-start.16 = (bf16[528,256]{1,0:T(8,128)(2,1)S(1)}, bf16[528,256]{1,0:T(8,128)(2,1)S(1)}, u32[]{:S(2)}, u32[]{:S(2)}) collective-permute-start(bf16[528,256]{1,0:T(8,128)(2,1)S(1)} %get-tuple-element.40), channel_id=1, source_target_pairs={{0,16},{4,20},{8,24},{12,28},{16,0},{20,4},{24,8},{28,12},{1,17},{... | collective-permute-start | bytes 811016 | tf_op jit(solution)/shard_map/ppermute | solution.py:520
  38.3 19.0 %collective-permute-start.17 = (bf16[528,256]{1,0:T(8,128)(2,1)S(1)}, bf16[528,256]{1,0:T(8,128)(2,1)S(1)}, u32[]{:S(2)}, u32[]{:S(2)}) collective-permute-start(bf16[528,256]{1,0:T(8,128)(2,1)S(1)} %get-tuple-element.41), channel_id=1, source_target_pairs={{0,20},{4,16},{8,28},{12,24},{16,4},{20,0},{24,12},{28,8},{1,21},{... | collective-permute-start | bytes 811016 | tf_op jit(solution)/shard_map/ppermute | solution.py:520
  39.3 7.5 %collective-permute-start.8 = (f32[2,128]{1,0:T(2,128)S(1)}, f32[2,128]{1,0:T(2,128)S(1)}, u32[]{:S(2)}, u32[]{:S(2)}) collective-permute-start(f32[2,128]{1,0:T(2,128)S(1)} %get-tuple-element.46), channel_id=1, source_target_pairs={{0,4},{4,0},{8,12},{12,8},{16,20},{20,16},{24,28},{28,24},{1,5},{5... | collective-permute-start | bytes 3080 | tf_op jit(solution)/shard_map/ppermute | solution.py:520
  40.2 7.4 %collective-permute-start.10 = (f32[2,128]{1,0:T(2,128)S(1)}, f32[2,128]{1,0:T(2,128)S(1)}, u32[]{:S(2)}, u32[]{:S(2)}) collective-permute-start(f32[2,128]{1,0:T(2,128)S(1)} %get-tuple-element.47), channel_id=1, source_target_pairs={{0,12},{4,8},{8,4},{12,0},{16,28},{20,24},{24,20},{28,16},{1,13},{... | collective-permute-start | bytes 3080 | tf_op jit(solution)/shard_map/ppermute | solution.py:520
  41.5 6.1 %collective-permute-start.9 = (f32[2,128]{1,0:T(2,128)S(1)}, f32[2,128]{1,0:T(2,128)S(1)}, u32[]{:S(2)}, u32[]{:S(2)}) collective-permute-start(f32[2,128]{1,0:T(2,128)S(1)} %get-tuple-element.48), channel_id=1, source_target_pairs={{0,8},{4,12},{8,0},{12,4},{16,24},{20,28},{24,16},{28,20},{1,9},{5... | collective-permute-start | bytes 3080 | tf_op jit(solution)/shard_map/ppermute | solution.py:520
  47.6 2.5 %collective-permute-start.11 = (f32[2,128]{1,0:T(2,128)S(1)}, f32[2,128]{1,0:T(2,128)S(1)}, u32[]{:S(2)}, u32[]{:S(2)}) collective-permute-start(f32[2,128]{1,0:T(2,128)S(1)} %fusion.2), channel_id=1, source_target_pairs={{0,1},{1,0},{2,3},{3,2},{4,5},{5,4},{6,7},{7,6},{8,9},{9,8},{10,11... | collective-permute-start | bytes 3080 | tf_op jit(solution)/shard_map/ppermute | solution.py:614
  50.1 5.2 %collective-permute-start.12 = (f32[2,128]{1,0:T(2,128)S(1)}, f32[2,128]{1,0:T(2,128)S(1)}, u32[]{:S(2)}, u32[]{:S(2)}) collective-permute-start(f32[2,128]{1,0:T(2,128)S(1)} %add.34), channel_id=1, source_target_pairs={{0,2},{1,3},{2,0},{3,1},{4,6},{5,7},{6,4},{7,5},{8,10},{9,11},{10,... | collective-permute-start | bytes 3080 | tf_op jit(solution)/shard_map/ppermute | solution.py:614
  52.4 14.9 %collective-permute-start.18 = (bf16[528,256]{1,0:T(8,128)(2,1)S(1)}, bf16[528,256]{1,0:T(8,128)(2,1)S(1)}, u32[]{:S(2)}, u32[]{:S(2)}) collective-permute-start(bf16[528,256]{1,0:T(8,128)(2,1)S(1)} %get-tuple-element.42), channel_id=1, source_target_pairs={{0,24},{4,28},{8,16},{12,20},{16,8},{20,12},{24,0},{28,4},{1,25},{... | collective-permute-start | bytes 811016 | tf_op jit(solution)/shard_map/ppermute | solution.py:520
  54.9 12.3 %collective-permute-start.19 = (bf16[528,256]{1,0:T(8,128)(2,1)S(1)}, bf16[528,256]{1,0:T(8,128)(2,1)S(1)}, u32[]{:S(2)}, u32[]{:S(2)}) collective-permute-start(bf16[528,256]{1,0:T(8,128)(2,1)S(1)} %get-tuple-element.43), channel_id=1, source_target_pairs={{0,28},{4,24},{8,20},{12,16},{16,12},{20,8},{24,4},{28,0},{1,29},{... | collective-permute-start | bytes 811016 | tf_op jit(solution)/shard_map/ppermute | solution.py:520
  55.3 12.0 %collective-permute-start.13 = (bf16[528,256]{1,0:T(8,128)(2,1)S(1)}, bf16[528,256]{1,0:T(8,128)(2,1)S(1)}, u32[]{:S(2)}, u32[]{:S(2)}) collective-permute-start(bf16[528,256]{1,0:T(8,128)(2,1)S(1)} %get-tuple-element.37), channel_id=1, source_target_pairs={{0,4},{4,0},{8,12},{12,8},{16,20},{20,16},{24,28},{28,24},{1,5},{5... | collective-permute-start | bytes 811016 | tf_op jit(solution)/shard_map/ppermute | solution.py:520
  56.1 23.2 %collective-permute-start.14 = (bf16[528,256]{1,0:T(8,128)(2,1)S(1)}, bf16[528,256]{1,0:T(8,128)(2,1)S(1)}, u32[]{:S(2)}, u32[]{:S(2)}) collective-permute-start(bf16[528,256]{1,0:T(8,128)(2,1)S(1)} %get-tuple-element.38), channel_id=1, source_target_pairs={{0,8},{4,12},{8,0},{12,4},{16,24},{20,28},{24,16},{28,20},{1,9},{5... | collective-permute-start | bytes 811016 | tf_op jit(solution)/shard_map/ppermute | solution.py:520
  57.3 22.0 %collective-permute-start.15 = (bf16[528,256]{1,0:T(8,128)(2,1)S(1)}, bf16[528,256]{1,0:T(8,128)(2,1)S(1)}, u32[]{:S(2)}, u32[]{:S(2)}) collective-permute-start(bf16[528,256]{1,0:T(8,128)(2,1)S(1)} %get-tuple-element.39), channel_id=1, source_target_pairs={{0,12},{4,8},{8,4},{12,0},{16,28},{20,24},{24,20},{28,16},{1,13},{... | collective-permute-start | bytes 811016 | tf_op jit(solution)/shard_map/ppermute | solution.py:520
where the time goes:
time: 82.1 us; the launch traced here: 81.9 us
  waiting for transfers between devices  42.9 us (52%)
  starting transfers between devices  23.4 us (29%)
  Pallas kernels  14.8 us (18%)
    ppermute x18, waiting for transfers between devices, swap_with(): return lax.ppermute(value, GROUP, pairs)  41.7 us
    ppermute x18, starting transfers between devices, swap_with(): return lax.ppermute(value, GROUP, pairs)  19.7 us
    pallas_call x1, Pallas kernels, fast_body(): pl.pallas_call(functools.partial(first_kernel, places, halves, rank), out...  5.06 us
    pallas_call x1, Pallas kernels, fast_body(): pl.pallas_call(functools.partial(weight_kernel, stations), out_shape=jax....  3.79 us
    ppermute x2, starting transfers between devices, fast_body(): power = power + lax.ppermute(power, 'channel', pairs)  3.67 us
    pallas_call x1, Pallas kernels, fast_body(): pl.pallas_call(functools.partial(finish_kernel, terms), out_shape=[jax.Sh...  2.5 us
    pallas_call x1, Pallas kernels, fast_body(): pl.pallas_call(pack_kernel, out_shape=[raw_block] * group, in_specs=[smem...  1.77 us
    pallas_call x1, Pallas kernels, fast_body(): pl.pallas_call(functools.partial(second_kernel, places), out_shape=[block...  1.71 us
  transfers between devices with their start and end apart: 20, of which 9 were waited for; matrix products, arithmetic and copies ran while one was open for 0% of the time, Pallas kernels for 5%

commit v1 on v0

--- a/solution.py
+++ b/solution.py
@@ -11,6 +11,7 @@
 ITERS = 3
 PHASES = 1024
 GROUP = ("tm", "station")
+EARLY = (0, 1, 2, 3, 4)
 
 
 HIGH = lax.Precision.HIGHEST
@@ -185,35 +186,37 @@
     return pltpu.CompilerParams(vmem_limit_bytes=mebibytes * 2**20)
 
 
-def pack_kernel(me_ref, volt_ref, seed_ref, *refs):
-    group = len(refs) - 3
-    outs, (held_ref, sem, seed_sem) = refs[:group], refs[group:]
+def pack_kernel(which, me_ref, volt_ref, seed_ref, *refs):
+    outs, (held_ref, sem, seed_sem) = refs[: len(which)], refs[len(which) :]
     me = me_ref[0]
     rows = volt_ref.shape[2]
-    seeds = pltpu.make_async_copy(seed_ref, held_ref, seed_sem)
-    seeds.start()
     copies = []
-    for place in range(group):
+    for line, place in enumerate(which):
+        channel = me ^ place
+        copies.append(
+            pltpu.make_async_copy(seed_ref.at[:, channel], held_ref.at[line], seed_sem.at[line])
+        )
+    for line, place in enumerate(which):
         for part in range(2):
-            copy = pltpu.make_async_copy(
-                volt_ref.at[part, me ^ place],
-                outs[place].at[pl.ds(part * rows, rows)],
-                sem.at[place, part],
+            copies.append(
+                pltpu.make_async_copy(
+                    volt_ref.at[part, me ^ place],
+                    outs[line].at[pl.ds(part * rows, rows)],
+                    sem.at[line, part],
+                )
             )
-            copy.start()
-            copies.append(copy)
+    for copy in copies:
+        copy.start()
     rank = seed_ref.shape[2] // 2
-    seeds.wait()
-    for place in range(group):
+    for line in range(len(which)):
+        copies[line].wait()
         halves = []
         for part in range(2):
-            pols = [
-                held_ref[part, me ^ place, pl.ds(pol, rank, stride=2), :] for pol in range(2)
-            ]
+            pols = [held_ref[line, part, pl.ds(pol, rank, stride=2), :] for pol in range(2)]
             halves.append(jnp.concatenate(pols, axis=1))
         start = jnp.concatenate(halves, axis=0).astype(jnp.float32)
-        outs[place][2 * rows :, :] = start.astype(jnp.bfloat16)
-    for copy in copies:
+        outs[line][2 * rows :, :] = start.astype(jnp.bfloat16)
+    for copy in copies[len(which) :]:
         copy.wait()
 
 
@@ -463,37 +466,42 @@
         power_ref[line : line + 1, :] = jnp.sum(sum_ref[line].T, axis=0, keepdims=True)
 
 
-def finish_kernel(terms, me_ref, power_ref, *refs):
-    *y, out_ref, base_ref, held, sem = refs
+def finish_kernel(terms, which, me_ref, power_ref, *refs):
+    y = refs[: len(which)]
+    out_ref, base_ref, held, kept, sem = refs[-5:]
     me = me_ref[0]
-    pols = power_ref.shape[0]
-    beams = power_ref.shape[1]
+    pols, beams = power_ref.shape
     rescale = lax.rsqrt(power_ref[...] * (1.0 / terms) + 1e-06)
     square = jnp.concatenate([rescale, jnp.zeros((beams - pols, beams), jnp.float32)], axis=0).T
     scale = [jnp.broadcast_to(square[:, pol : pol + 1], (beams, y[0].shape[1])) for pol in range(pols)]
     inputs = pols * beams
-    copies = []
-    for place, source in enumerate(y):
-        for part in range(2):
-            for pol in range(pols):
-                at = part * inputs + pol * beams
-                value = source[at : at + beams, :].astype(jnp.float32) * scale[pol]
-                held[place, part, pol * beams : (pol + 1) * beams, :] = value.astype(jnp.bfloat16)
-            copy = pltpu.make_async_copy(
-                held.at[place, part], out_ref.at[part, me ^ place], sem.at[place, part]
-            )
-            copy.start()
-            copies.append(copy)
     rows = (y[0].shape[0] - 2 * inputs) // 2
     rank = rows // 2
-    for place, source in enumerate(y):
+    copies = []
+    for line, place in enumerate(which):
+        source = y[line]
         both = source[2 * inputs :, :].astype(jnp.float32)
         value = both[:rows] + both[rows:]
         for part in range(2):
             for pol in range(pols):
-                base_ref[part, me ^ place, pl.ds(pol, rank, stride=pols), :] = value[
+                at = part * inputs + pol * beams
+                scaled = source[at : at + beams, :].astype(jnp.float32) * scale[pol]
+                held[line, part, pol * beams : (pol + 1) * beams, :] = scaled.astype(jnp.bfloat16)
+                kept[line, part, pl.ds(pol, rank, stride=pols), :] = value[
                     part * rank : (part + 1) * rank, pol * beams : (pol + 1) * beams
                 ]
+            copies.append(
+                pltpu.make_async_copy(
+                    held.at[line, part], out_ref.at[part, me ^ place], sem.at[line, part, 0]
+                )
+            )
+            copies[-1].start()
+            copies.append(
+                pltpu.make_async_copy(
+                    kept.at[line, part], base_ref.at[part, me ^ place], sem.at[line, part, 1]
+                )
+            )
+            copies[-1].start()
     for copy in copies:
         copy.wait()
 
@@ -519,27 +527,34 @@
         pairs = [(at, at ^ offset) for at in range(group)]
         return lax.ppermute(value, GROUP, pairs)
 
-    packed = pl.pallas_call(
-        pack_kernel,
-        out_shape=[raw_block] * group,
-        in_specs=[smem, hbm, hbm],
-        out_specs=[vmem] * group,
-        scratch_shapes=[
-            pltpu.VMEM((2, chan_count, rank * pols, stations), jnp.int32),
-            pltpu.SemaphoreType.DMA((group, 2)),
-            pltpu.SemaphoreType.DMA,
-        ],
-        compiler_params=room(6),
-        cost_estimate=pl.CostEstimate(
-            flops=0, transcendentals=0, bytes_accessed=4 * group * rows * times
-        ),
-    )(
-        me_array,
-        pltpu.with_memory_space_constraint(voltages.reshape(2, chan_count, inputs, times), HBM),
-        pltpu.with_memory_space_constraint(
-            start_seed.reshape(2, chan_count, rank * pols, stations), HBM
-        ),
-    )
+    volt_blocks = pltpu.with_memory_space_constraint(
+        voltages.reshape(2, chan_count, inputs, times), HBM
+    )
+    seed_blocks = pltpu.with_memory_space_constraint(
+        start_seed.reshape(2, chan_count, rank * pols, stations), HBM
+    )
+
+    def pack(which):
+        return pl.pallas_call(
+            functools.partial(pack_kernel, which),
+            out_shape=[raw_block] * len(which),
+            in_specs=[smem, hbm, hbm],
+            out_specs=[vmem] * len(which),
+            scratch_shapes=[
+                pltpu.VMEM((len(which), 2, rank * pols, stations), jnp.int32),
+                pltpu.SemaphoreType.DMA((len(which), 2)),
+                pltpu.SemaphoreType.DMA((len(which),)),
+            ],
+            compiler_params=room(4),
+            cost_estimate=pl.CostEstimate(
+                flops=0, transcendentals=0, bytes_accessed=4 * len(which) * rows * times
+            ),
+        )(me_array, volt_blocks, seed_blocks)
+
+    first_places = tuple(range(1, places))
+    other_places = tuple(range(places, group)) + (0,)
+    packed = dict(zip(first_places, pack(first_places)))
+    packed.update(zip(other_places, pack(other_places)))
     held = [packed[0]] + [swap_with(packed[o], o) for o in range(1, group)]
 
     total_stations = places * stations
@@ -608,30 +623,34 @@
     )
     back += [swap_with(late[o], places + o) for o in range(places)]
     slices = lax.axis_size("channel")
-    bit = 1
-    while bit < slices:
-        pairs = [(at, at ^ bit) for at in range(slices)]
-        power = power + lax.ppermute(power, "channel", pairs)
-        bit *= 2
+    own = power
+    for offset in range(1, slices):
+        pairs = [(at, at ^ offset) for at in range(slices)]
+        power = power + lax.ppermute(own, "channel", pairs)
 
     terms = float(chan_count * slices * times * halves)
-    beam_output, subspace = pl.pallas_call(
-        functools.partial(finish_kernel, terms),
-        out_shape=[
-            jax.ShapeDtypeStruct((2, chan_count, pols * beams, times), jnp.bfloat16),
-            jax.ShapeDtypeStruct((2, chan_count, rank * pols, stations), jnp.float32),
-        ],
-        in_specs=[smem] + [vmem] * (group + 1),
-        out_specs=[hbm, vmem],
-        scratch_shapes=[
-            pltpu.VMEM((group, 2, pols * beams, times), jnp.bfloat16),
-            pltpu.SemaphoreType.DMA((group, 2)),
-        ],
-        compiler_params=room(10),
-        cost_estimate=pl.CostEstimate(
-            flops=0, transcendentals=0, bytes_accessed=4 * group * rows * times
-        ),
-    )(me_array, power, *back)
+    outputs = []
+    for which in (EARLY, tuple(o for o in range(group) if o not in EARLY)):
+        outputs = pl.pallas_call(
+            functools.partial(finish_kernel, terms, which),
+            out_shape=[
+                jax.ShapeDtypeStruct((2, chan_count, pols * beams, times), jnp.bfloat16),
+                jax.ShapeDtypeStruct((2, chan_count, rank * pols, stations), jnp.float32),
+            ],
+            in_specs=[smem] + [vmem] * (len(which) + 1) + [hbm] * len(outputs),
+            out_specs=[hbm, hbm],
+            scratch_shapes=[
+                pltpu.VMEM((len(which), 2, pols * beams, times), jnp.bfloat16),
+                pltpu.VMEM((len(which), 2, rank * pols, stations), jnp.float32),
+                pltpu.SemaphoreType.DMA((len(which), 2, 2)),
+            ],
+            input_output_aliases={len(which) + 2 + at: at for at in range(len(outputs))},
+            compiler_params=room(8),
+            cost_estimate=pl.CostEstimate(
+                flops=0, transcendentals=0, bytes_accessed=4 * len(which) * rows * times
+            ),
+        )(me_array, power, *(back[o] for o in which), *outputs)
+    beam_output, subspace = outputs
     return (
         beam_output.reshape(2, chan_count, pols, beams, times),
         subspace.reshape(2, chan_count, rank, pols, stations),

time: 82.1 us -> 79.3 us (0.966)
  waiting for transfers between devices: 42.9 us -> 30.5 us
  starting transfers between devices: 23.4 us -> 31.5 us
  Pallas kernels: 14.8 us -> 16.3 us
    ppermute x18, waiting for transfers between devices: 41.7 us -> 29.9 us  [swap_with(): return lax.ppermute(value, GROUP, pairs)]
    ppermute x18, starting transfers between devices: 19.7 us -> 27.8 us  [swap_with(): return lax.ppermute(value, GROUP, pairs)]
    pallas_call x2 -> x4, Pallas kernels: 4.27 us -> 5.71 us  [the longest x2 2.87 us: pack(): pl.pallas_call(functools.partial(pack_kernel, which), out_shape=[raw_bloc...]
    ppermute x2 -> x3, starting transfers between devices: 3.67 us -> 3.74 us  [fast_body(): power = power + lax.ppermute(own, 'channel', pairs)]
  transfers between devices with their start and end apart: 20 -> 21, of which waited for: 9 -> 7; matrix products, arithmetic and copies ran while one was open for 0% -> 0% of each run, Pallas kernels for 5% -> 9%
where the time goes in v1:
time: 79.3 us; the launch traced here: 79.1 us
  starting transfers between devices  31.5 us (40%)
  waiting for transfers between devices  30.5 us (38%)
  Pallas kernels  16.3 us (21%)
    ppermute x18, waiting for transfers between devices, swap_with(): return lax.ppermute(value, GROUP, pairs)  29.9 us
    ppermute x18, starting transfers between devices, swap_with(): return lax.ppermute(value, GROUP, pairs)  27.8 us
    pallas_call x1, Pallas kernels, fast_body(): pl.pallas_call(functools.partial(first_kernel, places, halves, rank), out...  5.06 us
    pallas_call x1, Pallas kernels, fast_body(): pl.pallas_call(functools.partial(weight_kernel, stations), out_shape=jax....  3.79 us
    ppermute x3, starting transfers between devices, fast_body(): power = power + lax.ppermute(own, 'channel', pairs)  3.74 us
    pallas_call x2, Pallas kernels, pack(): pl.pallas_call(functools.partial(pack_kernel, which), out_shape=[raw_bloc...  2.87 us
    pallas_call x2, Pallas kernels, fast_body(): pl.pallas_call(functools.partial(finish_kernel, terms, which), out_shape=...  2.84 us
    pallas_call x1, Pallas kernels, fast_body(): pl.pallas_call(functools.partial(second_kernel, places), out_shape=[block...  1.7 us
  transfers between devices with their start and end apart: 21, of which 7 were waited for; matrix products, arithmetic and copies ran while one was open for 0% of the time, Pallas kernels for 9%

profile of v1, /device:TPU:1, one launch (start us, length us, event | category | flops | bytes accessed | tf_op | source)
XLA Modules:
  0.0 79.1 jit_solution(15701340268145728585)
XLA Ops:
  0.6 1.3 %shard_map.61 = (bf16[520,256]{1,0:T(8,128)(2,1)S(1)}, bf16[520,256]{1,0:T(8,128)(2,1)S(1)}, bf16[520,256]{1,0:T(8,128)(2,1)S(1)}) custom-call(s32[1]{0:T(128)} %bitcast.me_ref, bf16[2,8,256,256]{3,2,1,0:T(8,128)(2,1)} %bitcast.25, s32[2,8,8,128]{3,2,1,0:T(8,128)} %bitcast.28), custom_call_target="tpu_custom_call" | custom-call | bytes 1622016 | tf_op jit(solution)/shard_map/pallas_call | solution.py:538
  2.0 2.1 %collective-permute-start.4 = (bf16[520,256]{1,0:T(8,128)(2,1)S(1)}, bf16[520,256]{1,0:T(8,128)(2,1)S(1)}, u32[]{:S(2)}, u32[]{:S(2)}) collective-permute-start(bf16[520,256]{1,0:T(8,128)(2,1)S(1)} %get-tuple-element.31), channel_id=1, source_target_pairs={{0,4},{4,0},{8,12},{12,8},{16,20},{20,16},{24,28},{28,24},{1,5},{5... | collective-permute-start | bytes 798728 | tf_op jit(solution)/shard_map/ppermute | solution.py:528
  4.1 1.2 %collective-permute-start.5 = (bf16[520,256]{1,0:T(8,128)(2,1)S(1)}, bf16[520,256]{1,0:T(8,128)(2,1)S(1)}, u32[]{:S(2)}, u32[]{:S(2)}) collective-permute-start(bf16[520,256]{1,0:T(8,128)(2,1)S(1)} %get-tuple-element.32), channel_id=1, source_target_pairs={{0,8},{4,12},{8,0},{12,4},{16,24},{20,28},{24,16},{28,20},{1,9},{5... | collective-permute-start | bytes 798728 | tf_op jit(solution)/shard_map/ppermute | solution.py:528
  5.3 0.0 collective-permute-start.6
  5.3 1.5 %shard_map.59 = (bf16[520,256]{1,0:T(8,128)(2,1)S(1)}, bf16[520,256]{1,0:T(8,128)(2,1)S(1)}, bf16[520,256]{1,0:T(8,128)(2,1)S(1)}, bf16[520,256]{1,0:T(8,128)(2,1)S(1)}, bf16[520,256]{1,0:T(8,128)(2,1)S(1)}) custom-call(s32[1]{0:T(128)} %bitcast.me_ref, bf16[2,8,256,256]{3,2,1,0:T(8,128)(2,1)} %bitcast.26, s32[2,8,8,128]{3,2,1,0:T(8,128)} %bitcast.29), custom_call_target="tpu_custom_call" | custom-call | bytes 2703360 | tf_op jit(solution)/shard_map/pallas_call | solution.py:538
  6.9 1.3 %collective-permute-start = (bf16[520,256]{1,0:T(8,128)(2,1)S(1)}, bf16[520,256]{1,0:T(8,128)(2,1)S(1)}, u32[]{:S(2)}, u32[]{:S(2)}) collective-permute-start(bf16[520,256]{1,0:T(8,128)(2,1)S(1)} %get-tuple-element.26), channel_id=1, source_target_pairs={{0,16},{4,20},{8,24},{12,28},{16,0},{20,4},{24,8},{28,12},{1,17},{... | collective-permute-start | bytes 798728 | tf_op jit(solution)/shard_map/ppermute | solution.py:528
  8.2 1.6 %collective-permute-start.1 = (bf16[520,256]{1,0:T(8,128)(2,1)S(1)}, bf16[520,256]{1,0:T(8,128)(2,1)S(1)}, u32[]{:S(2)}, u32[]{:S(2)}) collective-permute-start(bf16[520,256]{1,0:T(8,128)(2,1)S(1)} %get-tuple-element.27), channel_id=1, source_target_pairs={{0,20},{4,16},{8,28},{12,24},{16,4},{20,0},{24,12},{28,8},{1,21},{... | collective-permute-start | bytes 798728 | tf_op jit(solution)/shard_map/ppermute | solution.py:528
  9.8 0.4 collective-permute-done.4.refs_1_
  10.2 3.8 %collective-permute-start.2 = (bf16[520,256]{1,0:T(8,128)(2,1)S(1)}, bf16[520,256]{1,0:T(8,128)(2,1)S(1)}, u32[]{:S(2)}, u32[]{:S(2)}) collective-permute-start(bf16[520,256]{1,0:T(8,128)(2,1)S(1)} %get-tuple-element.28), channel_id=1, source_target_pairs={{0,24},{4,28},{8,16},{12,20},{16,8},{20,12},{24,0},{28,4},{1,25},{... | collective-permute-start | bytes 798728 | tf_op jit(solution)/shard_map/ppermute | solution.py:528
  13.9 0.0 collective-permute-done.5.refs_2_
  13.9 5.3 %collective-permute-start.3 = (bf16[520,256]{1,0:T(8,128)(2,1)S(1)}, bf16[520,256]{1,0:T(8,128)(2,1)S(1)}, u32[]{:S(2)}, u32[]{:S(2)}) collective-permute-start(bf16[520,256]{1,0:T(8,128)(2,1)S(1)} %get-tuple-element.29), channel_id=1, source_target_pairs={{0,28},{4,24},{8,20},{12,16},{16,12},{20,8},{24,4},{28,0},{1,29},{... | collective-permute-start | bytes 798728 | tf_op jit(solution)/shard_map/ppermute | solution.py:528
  19.2 0.1 pad_add_fusion.scalars_ref
  19.3 3.8 %shard_map.60.refs_8_.refs_4_ = bf16[1024,1024]{1,0:T(8,128)(2,1)S(1)} custom-call(s32[2]{0:T(128)S(1)} %pad_add_fusion.scalars_ref, s32[512,512]{1,0:T(8,128)} %phase_ref.1, s32[1,512]{1,0:T(1,128)} %bitcast.31), custom_call_target="tpu_custom_call" | custom-call | flops 15728640 | bytes 3145728 | tf_op jit(solution)/shard_map/pallas_call | solution.py:562
  23.1 0.0 collective-permute-done.6.refs_3_
  23.1 0.0 collective-permute-done.refs_4_.refs_0_
  23.1 0.0 collective-permute-done.1.refs_5_.refs_1_
  23.1 6.2 %collective-permute-done.2.refs_6_.refs_2_ = bf16[520,256]{1,0:T(8,128)(2,1)S(1)} collective-permute-done((bf16[520,256]{1,0:T(8,128)(2,1)S(1)}, bf16[520,256]{1,0:T(8,128)(2,1)S(1)}, u32[]{:S(2)}, u32[]{:S(2)}) %collective-permute-start.2) | collective-permute-done | bytes 266272 | tf_op jit(solution)/shard_map/ppermute | solution.py:528
  29.3 0.0 collective-permute-done.3.refs_7_.refs_3_
  29.3 5.1 %shard_map.62 = (bf16[528,256]{1,0:T(8,128)(2,1)S(1)}, bf16[528,256]{1,0:T(8,128)(2,1)S(1)}, bf16[528,256]{1,0:T(8,128)(2,1)S(1)}, bf16[528,256]{1,0:T(8,128)(2,...) custom-call(bf16[520,256]{1,0:T(8,128)(2,1)S(1)} %get-tuple-element.30.refs_0_, ...), custom_call_target="tpu_custom_call" | custom-call | flops 2147483648 | bytes 3244032 | tf_op jit(solution)/shard_map/pallas_call | solution.py:589
  34.4 1.7 %shard_map.63 = (bf16[528,256]{1,0:T(8,128)(2,1)S(1)}, bf16[528,256]{1,0:T(8,128)(2,1)S(1)}, bf16[528,256]{1,0:T(8,128)(2,1)S(1)}, bf16[528,256]{1,0:T(8,128)(2,1)S(1)}, f32[8,128]{1,0:T(8,128)S(1)}) custom-call(bf16[520,256]{1,0:T(8,128)(2,1)S(1)} %collective-permute-done.refs_4_.refs_0_, bf16[520,256]{1,0:T(8,128)(2,1)S(1)} %collective-permute-done.1.refs_5_.refs_1_, ...), custom_call_target="tpu_custom_call" | custom-call | flops 1073741824 | bytes 2162688 | tf_op jit(solution)/shard_map/pallas_call | solution.py:606
  36.1 0.1 collective-permute-start.7
  36.2 0.5 collective-permute-start.20
  36.7 1.0 %collective-permute-start.17 = (bf16[528,256]{1,0:T(8,128)(2,1)S(1)}, bf16[528,256]{1,0:T(8,128)(2,1)S(1)}, u32[]{:S(2)}, u32[]{:S(2)}) collective-permute-start(bf16[528,256]{1,0:T(8,128)(2,1)S(1)} %get-tuple-element.42), channel_id=1, source_target_pairs={{0,4},{4,0},{8,12},{12,8},{16,20},{20,16},{24,28},{28,24},{1,5},{5... | collective-permute-start | bytes 811016 | tf_op jit(solution)/shard_map/ppermute | solution.py:528
  37.6 0.0 collective-permute-done.7
  37.6 0.7 collective-permute-start.8
  38.3 1.5 %collective-permute-start.10 = (f32[2,128]{1,0:T(2,128)S(1)}, f32[2,128]{1,0:T(2,128)S(1)}, u32[]{:S(2)}, u32[]{:S(2)}) collective-permute-start(f32[2,128]{1,0:T(2,128)S(1)} %get-tuple-element.51), channel_id=1, source_target_pairs={{0,12},{4,8},{8,4},{12,0},{16,28},{20,24},{24,20},{28,16},{1,13},{... | collective-permute-start | bytes 3080 | tf_op jit(solution)/shard_map/ppermute | solution.py:528
  39.8 0.5 collective-permute-start.9
  40.3 4.3 %collective-permute-done.8 = f32[2,128]{1,0:T(2,128)S(1)} collective-permute-done((f32[2,128]{1,0:T(2,128)S(1)}, f32[2,128]{1,0:T(2,128)S(1)}, u32[]{:S(2)}, u32[]{:S(2)}) %collective-permute-start.8) | collective-permute-done | bytes 1056 | tf_op jit(solution)/shard_map/ppermute | solution.py:528
  44.6 0.7 collective-permute-done.10
  45.3 0.0 collective-permute-done.9
  45.3 3.4 %collective-permute-start.13 = (f32[2,128]{1,0:T(2,128)S(1)}, f32[2,128]{1,0:T(2,128)S(1)}, u32[]{:S(2)}, u32[]{:S(2)}) collective-permute-start(f32[2,128]{1,0:T(2,128)S(1)} %fusion.2), channel_id=1, source_target_pairs={{0,3},{1,2},{2,1},{3,0},{4,7},{5,6},{6,5},{7,4},{8,11},{9,10},{10,... | collective-permute-start | bytes 3080 | tf_op jit(solution)/shard_map/ppermute | solution.py:629
  48.7 0.0 collective-permute-start.12
  48.7 0.4 collective-permute-start.11
  49.1 0.6 collective-permute-done.13
  49.7 2.5 %collective-permute-start.14 = (bf16[528,256]{1,0:T(8,128)(2,1)S(1)}, bf16[528,256]{1,0:T(8,128)(2,1)S(1)}, u32[]{:S(2)}, u32[]{:S(2)}) collective-permute-start(bf16[528,256]{1,0:T(8,128)(2,1)S(1)} %get-tuple-element.38), channel_id=1, source_target_pairs={{0,20},{4,16},{8,28},{12,24},{16,4},{20,0},{24,12},{28,8},{1,21},{... | collective-permute-start | bytes 811016 | tf_op jit(solution)/shard_map/ppermute | solution.py:528
  52.1 0.0 collective-permute-done.12
  52.2 0.9 %collective-permute-start.18 = (bf16[528,256]{1,0:T(8,128)(2,1)S(1)}, bf16[528,256]{1,0:T(8,128)(2,1)S(1)}, u32[]{:S(2)}, u32[]{:S(2)}) collective-permute-start(bf16[528,256]{1,0:T(8,128)(2,1)S(1)} %get-tuple-element.43), channel_id=1, source_target_pairs={{0,8},{4,12},{8,0},{12,4},{16,24},{20,28},{24,16},{28,20},{1,9},{5... | collective-permute-start | bytes 811016 | tf_op jit(solution)/shard_map/ppermute | solution.py:528
  53.1 0.0 collective-permute-done.11
  53.1 1.5 %collective-permute-start.19 = (bf16[528,256]{1,0:T(8,128)(2,1)S(1)}, bf16[528,256]{1,0:T(8,128)(2,1)S(1)}, u32[]{:S(2)}, u32[]{:S(2)}) collective-permute-start(bf16[528,256]{1,0:T(8,128)(2,1)S(1)} %get-tuple-element.44), channel_id=1, source_target_pairs={{0,12},{4,8},{8,4},{12,0},{16,28},{20,24},{24,20},{28,16},{1,13},{... | collective-permute-start | bytes 811016 | tf_op jit(solution)/shard_map/ppermute | solution.py:528
  54.6 0.0 collective-permute-done.20.refs_4_
  54.6 3.0 %collective-permute-start.15 = (bf16[528,256]{1,0:T(8,128)(2,1)S(1)}, bf16[528,256]{1,0:T(8,128)(2,1)S(1)}, u32[]{:S(2)}, u32[]{:S(2)}) collective-permute-start(bf16[528,256]{1,0:T(8,128)(2,1)S(1)} %get-tuple-element.39), channel_id=1, source_target_pairs={{0,24},{4,28},{8,16},{12,20},{16,8},{20,12},{24,0},{28,4},{1,25},{... | collective-permute-start | bytes 811016 | tf_op jit(solution)/shard_map/ppermute | solution.py:528
  57.5 0.0 collective-permute-done.17.refs_1_
  57.5 0.4 collective-permute-start.16
  57.9 0.0 collective-permute-done.18.refs_2_
  57.9 8.1 %collective-permute-done.19.refs_3_ = bf16[528,256]{1,0:T(8,128)(2,1)S(1)} collective-permute-done((bf16[528,256]{1,0:T(8,128)(2,1)S(1)}, bf16[528,256]{1,0:T(8,128)(2,1)S(1)}, u32[]{:S(2)}, u32[]{:S(2)}) %collective-permute-start.19) | collective-permute-done | bytes 270368 | tf_op jit(solution)/shard_map/ppermute | solution.py:528
  66.0 1.6 %shard_map.64 = (bf16[2,8,256,256]{3,2,1,0:T(8,128)(2,1)}, f32[2,8,8,128]{3,2,1,0:T(8,128)}) custom-call(s32[1]{0:T(128)} %bitcast.me_ref, f32[2,128]{1,0:T(2,128)S(1)} %add_add_fusion.power_ref, bf16[528,256]{1,0:T(8,128)(2,1)S(1)} %get-tuple-element.41.refs_0_, bf16[528,256]{1,0:T(8,128)(2,1)S(1)} %collective-permute-done.17.refs_1_, ...), custom_call_target="tpu_custom_call" | custom-call | bytes 2703360 | tf_op jit(solution)/shard_map/pallas_call | solution.py:634
  67.6 0.0 collective-permute-done.14.refs_0_
  67.6 10.2 %collective-permute-done.15.refs_1_ = bf16[528,256]{1,0:T(8,128)(2,1)S(1)} collective-permute-done((bf16[528,256]{1,0:T(8,128)(2,1)S(1)}, bf16[528,256]{1,0:T(8,128)(2,1)S(1)}, u32[]{:S(2)}, u32[]{:S(2)}) %collective-permute-start.15) | collective-permute-done | bytes 270368 | tf_op jit(solution)/shard_map/ppermute | solution.py:528
  77.9 0.0 collective-permute-done.16.refs_2_
  77.9 1.3 %shard_map.65 = (bf16[2,8,256,256]{3,2,1,0:T(8,128)(2,1)}, f32[2,8,8,128]{3,2,1,0:T(8,128)}) custom-call(s32[1]{0:T(128)} %bitcast.me_ref, f32[2,128]{1,0:T(2,128)S(1)} %add_add_fusion.power_ref, bf16[528,256]{1,0:T(8,128)(2,1)S(1)} %collective-permute-done.14.refs_0_, ...), custom_call_target="tpu_custom_call", output_to_operand_aliasing={{0}: (5, {}), {1}: (6, {})} | custom-call | bytes 1622016 | tf_op jit(solution)/shard_map/pallas_call | solution.py:634
  (4 shorter events, 0.0 us)
Async XLA Ops:
  2.0 8.2 %collective-permute-start.4 = (bf16[520,256]{1,0:T(8,128)(2,1)S(1)}, bf16[520,256]{1,0:T(8,128)(2,1)S(1)}, u32[]{:S(2)}, u32[]{:S(2)}) collective-permute-start(bf16[520,256]{1,0:T(8,128)(2,1)S(1)} %get-tuple-element.31), channel_id=1, source_target_pairs={{0,4},{4,0},{8,12},{12,8},{16,20},{20,16},{24,28},{28,24},{1,5},{5... | collective-permute-start | bytes 798728 | tf_op jit(solution)/shard_map/ppermute | solution.py:528
  4.1 9.9 %collective-permute-start.5 = (bf16[520,256]{1,0:T(8,128)(2,1)S(1)}, bf16[520,256]{1,0:T(8,128)(2,1)S(1)}, u32[]{:S(2)}, u32[]{:S(2)}) collective-permute-start(bf16[520,256]{1,0:T(8,128)(2,1)S(1)} %get-tuple-element.32), channel_id=1, source_target_pairs={{0,8},{4,12},{8,0},{12,4},{16,24},{20,28},{24,16},{28,20},{1,9},{5... | collective-permute-start | bytes 798728 | tf_op jit(solution)/shard_map/ppermute | solution.py:528
  5.3 17.8 %collective-permute-start.6 = (bf16[520,256]{1,0:T(8,128)(2,1)S(1)}, bf16[520,256]{1,0:T(8,128)(2,1)S(1)}, u32[]{:S(2)}, u32[]{:S(2)}) collective-permute-start(bf16[520,256]{1,0:T(8,128)(2,1)S(1)} %get-tuple-element.33), channel_id=1, source_target_pairs={{0,12},{4,8},{8,4},{12,0},{16,28},{20,24},{24,20},{28,16},{1,13},{... | collective-permute-start | bytes 798728 | tf_op jit(solution)/shard_map/ppermute | solution.py:528
  6.9 16.2 %collective-permute-start = (bf16[520,256]{1,0:T(8,128)(2,1)S(1)}, bf16[520,256]{1,0:T(8,128)(2,1)S(1)}, u32[]{:S(2)}, u32[]{:S(2)}) collective-permute-start(bf16[520,256]{1,0:T(8,128)(2,1)S(1)} %get-tuple-element.26), channel_id=1, source_target_pairs={{0,16},{4,20},{8,24},{12,28},{16,0},{20,4},{24,8},{28,12},{1,17},{... | collective-permute-start | bytes 798728 | tf_op jit(solution)/shard_map/ppermute | solution.py:528
  8.2 14.9 %collective-permute-start.1 = (bf16[520,256]{1,0:T(8,128)(2,1)S(1)}, bf16[520,256]{1,0:T(8,128)(2,1)S(1)}, u32[]{:S(2)}, u32[]{:S(2)}) collective-permute-start(bf16[520,256]{1,0:T(8,128)(2,1)S(1)} %get-tuple-element.27), channel_id=1, source_target_pairs={{0,20},{4,16},{8,28},{12,24},{16,4},{20,0},{24,12},{28,8},{1,21},{... | collective-permute-start | bytes 798728 | tf_op jit(solution)/shard_map/ppermute | solution.py:528
  10.2 19.1 %collective-permute-start.2 = (bf16[520,256]{1,0:T(8,128)(2,1)S(1)}, bf16[520,256]{1,0:T(8,128)(2,1)S(1)}, u32[]{:S(2)}, u32[]{:S(2)}) collective-permute-start(bf16[520,256]{1,0:T(8,128)(2,1)S(1)} %get-tuple-element.28), channel_id=1, source_target_pairs={{0,24},{4,28},{8,16},{12,20},{16,8},{20,12},{24,0},{28,4},{1,25},{... | collective-permute-start | bytes 798728 | tf_op jit(solution)/shard_map/ppermute | solution.py:528
  13.9 15.4 %collective-permute-start.3 = (bf16[520,256]{1,0:T(8,128)(2,1)S(1)}, bf16[520,256]{1,0:T(8,128)(2,1)S(1)}, u32[]{:S(2)}, u32[]{:S(2)}) collective-permute-start(bf16[520,256]{1,0:T(8,128)(2,1)S(1)} %get-tuple-element.29), channel_id=1, source_target_pairs={{0,28},{4,24},{8,20},{12,16},{16,12},{20,8},{24,4},{28,0},{1,29},{... | collective-permute-start | bytes 798728 | tf_op jit(solution)/shard_map/ppermute | solution.py:528
  36.1 1.5 %collective-permute-start.7 = (f32[4,2,128]{2,1,0:T(2,128)S(1)}, f32[4,2,128]{2,1,0:T(2,128)S(1)}, u32[]{:S(2)}, u32[]{:S(2)}) collective-permute-start(f32[4,2,128]{2,1,0:T(2,128)S(1)} %bitcast.23), channel_id=1, source_target_pairs={{0,16},{4,20},{8,24},{12,28},{16,0},{20,4},{24,8},{28,12},{1,17},{... | collective-permute-start | bytes 12296 | tf_op jit(solution)/shard_map/ppermute | solution.py:528
  36.2 18.4 %collective-permute-start.20 = (bf16[528,256]{1,0:T(8,128)(2,1)S(1)}, bf16[528,256]{1,0:T(8,128)(2,1)S(1)}, u32[]{:S(2)}, u32[]{:S(2)}) collective-permute-start(bf16[528,256]{1,0:T(8,128)(2,1)S(1)} %get-tuple-element.45), channel_id=1, source_target_pairs={{0,16},{4,20},{8,24},{12,28},{16,0},{20,4},{24,8},{28,12},{1,17},{... | collective-permute-start | bytes 811016 | tf_op jit(solution)/shard_map/ppermute | solution.py:528
  36.7 20.9 %collective-permute-start.17 = (bf16[528,256]{1,0:T(8,128)(2,1)S(1)}, bf16[528,256]{1,0:T(8,128)(2,1)S(1)}, u32[]{:S(2)}, u32[]{:S(2)}) collective-permute-start(bf16[528,256]{1,0:T(8,128)(2,1)S(1)} %get-tuple-element.42), channel_id=1, source_target_pairs={{0,4},{4,0},{8,12},{12,8},{16,20},{20,16},{24,28},{28,24},{1,5},{5... | collective-permute-start | bytes 811016 | tf_op jit(solution)/shard_map/ppermute | solution.py:528
  37.6 7.0 %collective-permute-start.8 = (f32[2,128]{1,0:T(2,128)S(1)}, f32[2,128]{1,0:T(2,128)S(1)}, u32[]{:S(2)}, u32[]{:S(2)}) collective-permute-start(f32[2,128]{1,0:T(2,128)S(1)} %get-tuple-element.50), channel_id=1, source_target_pairs={{0,4},{4,0},{8,12},{12,8},{16,20},{20,16},{24,28},{28,24},{1,5},{5... | collective-permute-start | bytes 3080 | tf_op jit(solution)/shard_map/ppermute | solution.py:528
  38.3 7.0 %collective-permute-start.10 = (f32[2,128]{1,0:T(2,128)S(1)}, f32[2,128]{1,0:T(2,128)S(1)}, u32[]{:S(2)}, u32[]{:S(2)}) collective-permute-start(f32[2,128]{1,0:T(2,128)S(1)} %get-tuple-element.51), channel_id=1, source_target_pairs={{0,12},{4,8},{8,4},{12,0},{16,28},{20,24},{24,20},{28,16},{1,13},{... | collective-permute-start | bytes 3080 | tf_op jit(solution)/shard_map/ppermute | solution.py:528
  39.8 5.5 %collective-permute-start.9 = (f32[2,128]{1,0:T(2,128)S(1)}, f32[2,128]{1,0:T(2,128)S(1)}, u32[]{:S(2)}, u32[]{:S(2)}) collective-permute-start(f32[2,128]{1,0:T(2,128)S(1)} %get-tuple-element.52), channel_id=1, source_target_pairs={{0,8},{4,12},{8,0},{12,4},{16,24},{20,28},{24,16},{28,20},{1,9},{5... | collective-permute-start | bytes 3080 | tf_op jit(solution)/shard_map/ppermute | solution.py:528
  45.3 4.3 %collective-permute-start.13 = (f32[2,128]{1,0:T(2,128)S(1)}, f32[2,128]{1,0:T(2,128)S(1)}, u32[]{:S(2)}, u32[]{:S(2)}) collective-permute-start(f32[2,128]{1,0:T(2,128)S(1)} %fusion.2), channel_id=1, source_target_pairs={{0,3},{1,2},{2,1},{3,0},{4,7},{5,6},{6,5},{7,4},{8,11},{9,10},{10,... | collective-permute-start | bytes 3080 | tf_op jit(solution)/shard_map/ppermute | solution.py:629
  48.7 3.4 %collective-permute-start.12 = (f32[2,128]{1,0:T(2,128)S(1)}, f32[2,128]{1,0:T(2,128)S(1)}, u32[]{:S(2)}, u32[]{:S(2)}) collective-permute-start(f32[2,128]{1,0:T(2,128)S(1)} %fusion.2), channel_id=1, source_target_pairs={{0,2},{1,3},{2,0},{3,1},{4,6},{5,7},{6,4},{7,5},{8,10},{9,11},{10,... | collective-permute-start | bytes 3080 | tf_op jit(solution)/shard_map/ppermute | solution.py:629
  48.7 4.4 %collective-permute-start.11 = (f32[2,128]{1,0:T(2,128)S(1)}, f32[2,128]{1,0:T(2,128)S(1)}, u32[]{:S(2)}, u32[]{:S(2)}) collective-permute-start(f32[2,128]{1,0:T(2,128)S(1)} %fusion.2), channel_id=1, source_target_pairs={{0,1},{1,0},{2,3},{3,2},{4,5},{5,4},{6,7},{7,6},{8,9},{9,8},{10,11... | collective-permute-start | bytes 3080 | tf_op jit(solution)/shard_map/ppermute | solution.py:629
  49.7 17.9 %collective-permute-start.14 = (bf16[528,256]{1,0:T(8,128)(2,1)S(1)}, bf16[528,256]{1,0:T(8,128)(2,1)S(1)}, u32[]{:S(2)}, u32[]{:S(2)}) collective-permute-start(bf16[528,256]{1,0:T(8,128)(2,1)S(1)} %get-tuple-element.38), channel_id=1, source_target_pairs={{0,20},{4,16},{8,28},{12,24},{16,4},{20,0},{24,12},{28,8},{1,21},{... | collective-permute-start | bytes 811016 | tf_op jit(solution)/shard_map/ppermute | solution.py:528
  52.2 5.8 %collective-permute-start.18 = (bf16[528,256]{1,0:T(8,128)(2,1)S(1)}, bf16[528,256]{1,0:T(8,128)(2,1)S(1)}, u32[]{:S(2)}, u32[]{:S(2)}) collective-permute-start(bf16[528,256]{1,0:T(8,128)(2,1)S(1)} %get-tuple-element.43), channel_id=1, source_target_pairs={{0,8},{4,12},{8,0},{12,4},{16,24},{20,28},{24,16},{28,20},{1,9},{5... | collective-permute-start | bytes 811016 | tf_op jit(solution)/shard_map/ppermute | solution.py:528
  53.1 13.0 %collective-permute-start.19 = (bf16[528,256]{1,0:T(8,128)(2,1)S(1)}, bf16[528,256]{1,0:T(8,128)(2,1)S(1)}, u32[]{:S(2)}, u32[]{:S(2)}) collective-permute-start(bf16[528,256]{1,0:T(8,128)(2,1)S(1)} %get-tuple-element.44), channel_id=1, source_target_pairs={{0,12},{4,8},{8,4},{12,0},{16,28},{20,24},{24,20},{28,16},{1,13},{... | collective-permute-start | bytes 811016 | tf_op jit(solution)/shard_map/ppermute | solution.py:528
  54.6 23.3 %collective-permute-start.15 = (bf16[528,256]{1,0:T(8,128)(2,1)S(1)}, bf16[528,256]{1,0:T(8,128)(2,1)S(1)}, u32[]{:S(2)}, u32[]{:S(2)}) collective-permute-start(bf16[528,256]{1,0:T(8,128)(2,1)S(1)} %get-tuple-element.39), channel_id=1, source_target_pairs={{0,24},{4,28},{8,16},{12,20},{16,8},{20,12},{24,0},{28,4},{1,25},{... | collective-permute-start | bytes 811016 | tf_op jit(solution)/shard_map/ppermute | solution.py:528
  57.5 20.3 %collective-permute-start.16 = (bf16[528,256]{1,0:T(8,128)(2,1)S(1)}, bf16[528,256]{1,0:T(8,128)(2,1)S(1)}, u32[]{:S(2)}, u32[]{:S(2)}) collective-permute-start(bf16[528,256]{1,0:T(8,128)(2,1)S(1)} %get-tuple-element.40), channel_id=1, source_target_pairs={{0,28},{4,24},{8,20},{12,16},{16,12},{20,8},{24,4},{28,0},{1,29},{... | collective-permute-start | bytes 811016 | tf_op jit(solution)/shard_map/ppermute | solution.py:528
